TPU v7x, 512 devices: a whole 4x8x8 slice. The times are simulated.
512 devices in a mesh: blk: 64 (over x, y_lo, z), rep: 8 (over y_hi, core).
Axes of the slice: x: 4, y: 8 (y_hi: 4, y_lo: 2; y = y_hi * 2 + y_lo), z: 8, core: 2. Of those that a mesh axis runs over, the one named last changes fastest.
Arguments:
- position: float32 [3, 524288], P(None, 'blk'), may hold values from -6 to 6
- velocity: float32 [3, 524288], P(None, 'blk'), may hold values from -6 to 6
- accel: float32 [3, 524288], P(None, 'blk'), may hold values from -6 to 6
- jerk: float32 [3, 524288], P(None, 'blk'), may hold values from -12 to 12
- mass: float32 [524288], P('blk'), may hold values from 0.1 to 10
- elapsed: float32 [524288], P('blk'), may hold values from 0.02 to 0.25
- active_index: int32 [16384], P('blk'), may hold values from -1 to 524287, as said below
Outputs:
- force: float32 [3, 16384], P(None, 'blk')
- new_jerk: float32 [3, 16384], P(None, 'blk')
Inputs may be any that keep to these rules, and one draw needn't show every extreme that they name: `active_index`: each team t has 256 slots; they hold the indices of active stars of that team (t * 8192 to (t + 1) * 8192 - 1) in increasing order, then -1 in the remaining slots. Every team has at least one active star, and in every draw some team has all 256 slots filled; the counts differ strongly from team to team.
All inputs are finite; a program needn't handle non-finite values.
Results may differ from a plain program's by a relative error of at most 0.0003.
Values sent between devices are 32-bit elements; how exact they have to be, the bound alone decides.
A program may use at most 64 MiB of HBM per device.

v0:
```python
import math

import jax
import jax.numpy as jnp
from jax import lax
from jax.sharding import PartitionSpec as P

SOFTENING = 0.001


def shifted(value, axis, by):
    size = lax.axis_size(axis)
    return lax.ppermute(value, axis, [(i, (i + by) % size) for i in range(size)])


def predict(position, velocity, accel, jerk, elapsed):
    step_time = elapsed[None, :]
    moved = position + step_time * (velocity + step_time * (0.5 * accel + step_time / 6.0 * jerk))
    turned = velocity + step_time * (accel + 0.5 * step_time * jerk)
    return (moved, turned)


def pair_sums(targets, sources, weights):
    delta_one = sources[0][None, :] - targets[0][:, None]
    delta_two = sources[1][None, :] - targets[1][:, None]
    delta_three = sources[2][None, :] - targets[2][:, None]
    drift_one = sources[3][None, :] - targets[3][:, None]
    drift_two = sources[4][None, :] - targets[4][:, None]
    drift_three = sources[5][None, :] - targets[5][:, None]
    radius_sq = (
        delta_one * delta_one + delta_two * delta_two + delta_three * delta_three + SOFTENING
    )
    inverse = lax.rsqrt(radius_sq)
    strength = weights[None, :] * inverse * inverse * inverse
    radial = (
        3.0
        * (delta_one * drift_one + delta_two * drift_two + delta_three * drift_three)
        * (inverse * inverse)
    )
    pull_one = jnp.sum(strength * delta_one, axis=1)
    pull_two = jnp.sum(strength * delta_two, axis=1)
    pull_three = jnp.sum(strength * delta_three, axis=1)
    twist_one = jnp.sum(strength * (drift_one - radial * delta_one), axis=1)
    twist_two = jnp.sum(strength * (drift_two - radial * delta_two), axis=1)
    twist_three = jnp.sum(strength * (drift_three - radial * delta_three), axis=1)
    return jnp.stack([pull_one, pull_two, pull_three, twist_one, twist_two, twist_three], 0)


def tile_sums(targets, block):
    rows = targets.shape[1]
    width = block.shape[1]
    step = math.gcd(width, max(128, 1048576 // rows))

    def add_piece(piece_no, total):
        piece = lax.dynamic_slice_in_dim(block, piece_no * step, step, 1)
        return total + pair_sums(targets, piece, piece[6])

    return lax.fori_loop(0, width // step, add_piece, jnp.zeros((6, rows), jnp.float32))


def live_sums(total, targets, block, live, rows):
    needed = (live + rows - 1) // rows

    def add_rows(block_no, running):
        return running + tile_sums(targets, block)

    return lax.fori_loop(0, needed, add_rows, total)


def cycle_sums(targets, live, block, turns):
    rows = targets.shape[1]

    def advance(turn_no, carry):
        total, current = carry
        total = live_sums(total, targets, current, live, rows)
        return (total, shifted(current, "blk", 1))

    start = jnp.zeros(targets.shape, jnp.float32)
    total, current = lax.fori_loop(0, turns - 1, advance, (start, block))
    return live_sums(total, targets, current, live, rows)


def skewed(block, span):
    replica = lax.axis_index("rep")
    for bit_no in range((lax.axis_size("rep") - 1).bit_length()):
        moved = shifted(block, "blk", span * (1 << bit_no))
        block = jnp.where(replica // (1 << bit_no) % 2 == 1, moved, block)
    return block


def replica_total(sums):
    return lax.psum(sums, "rep")


def body(position, velocity, accel, jerk, mass, elapsed, active_index):
    teams = lax.axis_size("blk")
    replicas = lax.axis_size("rep")
    team = lax.axis_index("blk")
    stars_dev = position.shape[1]
    moved, turned = predict(position, velocity, accel, jerk, elapsed)
    field = jnp.concatenate([moved, turned, mass[None, :]], 0)
    live_mask = active_index >= 0
    own_count = jnp.sum(live_mask.astype(jnp.int32))
    local = jnp.clip(active_index - team * stars_dev, 0, stars_dev - 1)
    own_rows = jnp.take(field[0:6], local, axis=1)
    span = teams // replicas
    sums = cycle_sums(own_rows, own_count, skewed(field, span), span)
    sums = replica_total(sums)
    scaled = jnp.where(live_mask[None, :], sums / (stars_dev * teams), 0.0)
    return (scaled[0:3], scaled[3:6])


def solution(mesh):
    in_specs = (
        P(None, "blk"),
        P(None, "blk"),
        P(None, "blk"),
        P(None, "blk"),
        P("blk"),
        P("blk"),
        P("blk"),
    )
    out_specs = (P(None, "blk"), P(None, "blk"))
    return jax.shard_map(body, mesh=mesh, in_specs=in_specs, out_specs=out_specs, check_vma=False)
```

profile of v0, /device:TPU:1, one launch (start us, length us, event | category | flops | bytes accessed | tf_op | source)
XLA Modules:
  0.0 227.7 jit_solution(5129332223691011271)
XLA Ops:
  3.5 4.0 %collective-permute-start.1 = (f32[7,8192]{1,0:T(8,128)S(1)}, f32[7,8192]{1,0:T(8,128)S(1)}, u32[]{:S(2)}, u32[]{:S(2)}) collective-permute-start(f32[7,8192]{1,0:T(8,128)S(1)} %pad_maximum_fusion), channel_id=1, source_target_pairs={{0,64},{8,72},{16,80},{24,88},{32,96},{40,104},{48,112},{56,120},{... | collective-permute-start | bytes 688136 | tf_op jit(solution)/shard_map/ppermute | solution.py:13
  9.7 2.6 %copy.43 = f32[6,8192]{0,1:T(8,128)} copy(f32[6,8192]{1,0:T(8,128)S(1)} %pad_maximum_fusion.1) | data formatting | bytes 393216 | tf_op jit(solution)/shard_map/concatenate | solution.py:101
  13.6 3.9 %collective-permute-start.2 = (f32[7,8192]{1,0:T(8,128)S(1)}, f32[7,8192]{1,0:T(8,128)S(1)}, u32[]{:S(2)}, u32[]{:S(2)}) collective-permute-start(f32[7,8192]{1,0:T(8,128)S(1)} %broadcast_select_fusion), channel_id=1, source_target_pairs={{0,128},{8,136},{16,144},{24,152},{32,160},{40,168},{48,176},{56,1... | collective-permute-start | bytes 688136 | tf_op jit(solution)/shard_map/ppermute | solution.py:13
  17.6 2.9 %gather_fusion = f32[256,6]{1,0:T(8,128)S(1)} fusion(f32[6,8192]{0,1:T(8,128)} %copy.43, s32[1024]{0:T(1024)S(1)} %pad_clamp_fusion), kind=kCustom, calls=%fused_computation | custom fusion | bytes 13312 | tf_op jit(solution)/shard_map/jit(_take)/gather | solution.py:105
  20.5 2.3 %collective-permute-done.2 = f32[7,8192]{1,0:T(8,128)S(1)} collective-permute-done((f32[7,8192]{1,0:T(8,128)S(1)}, f32[7,8192]{1,0:T(8,128)S(1)}, u32[]{:S(2)}, u32[]{:S(2)}) %collective-permute-start.2) | collective-permute-done | bytes 229408 | tf_op jit(solution)/shard_map/ppermute | solution.py:13
  22.9 4.5 %collective-permute-start.3 = (f32[7,8192]{1,0:T(8,128)S(1)}, f32[7,8192]{1,0:T(8,128)S(1)}, u32[]{:S(2)}, u32[]{:S(2)}) collective-permute-start(f32[7,8192]{1,0:T(8,128)S(1)} %broadcast_select_fusion.1), channel_id=1, source_target_pairs={{0,256},{8,264},{16,272},{24,280},{32,288},{40,296},{48,304},{56,3... | collective-permute-start | bytes 688136 | tf_op jit(solution)/shard_map/ppermute | solution.py:13
  27.5 4.1 %collective-permute-done.3 = f32[7,8192]{1,0:T(8,128)S(1)} collective-permute-done((f32[7,8192]{1,0:T(8,128)S(1)}, f32[7,8192]{1,0:T(8,128)S(1)}, u32[]{:S(2)}, u32[]{:S(2)}) %collective-permute-start.3) | collective-permute-done | bytes 229408 | tf_op jit(solution)/shard_map/ppermute | solution.py:13
  31.6 160.5 %while.72 = (s32[]{:T(128)}, f32[6,256]{1,0:T(8,128)S(1)}, f32[7,8192]{1,0:T(8,128)S(1)}, s32[]{:T(128)}, f32[6,256]{1,0:T(8,128)S(1)}, /*index=5*/s32[]{:T(128)...) while((s32[]{:T(128)}, f32[6,256]{1,0:T(8,128)S(1)}, ...), condition=%wide.region_12.13_spmd, body=%wide.region_1.12_spmd.sunk | while | flops 42994700 | bytes 1794971 | solution.py:79
  32.3 6.1 %collective-permute-start = (f32[7,8192]{1,0:T(8,128)}, f32[7,8192]{1,0:T(8,128)S(1)}, u32[]{:S(2)}, u32[]{:S(2)}) collective-permute-start(f32[7,8192]{1,0:T(8,128)} %copy.69), channel_id=1, source_target_pairs={{0,8},{8,16},{16,24},{24,32},{32,40},{40,48},{48,56},{56,64},{64,7... | collective-permute-start | bytes 688136 | tf_op jit(solution)/shard_map/while/body/eval_jaxpr/ppermute | solution.py:13
  38.5 18.1 %while.75 = (s32[]{:T(128)}, f32[6,256]{1,0:T(8,128)S(1)}, s32[]{:T(128)}, f32[7,8192]{1,0:T(8,128)}, f32[6,256]{1,0:T(8,128)S(1)}, /*index=5*/s32[]{:T(128)}, s...) while((s32[]{:T(128)}, f32[6,256]{1,0:T(8,128)S(1)}, ...), condition=%wide.region_11.11_spmd, body=%wide.region_2.10_spmd.sunk | while | flops 42994700 | bytes 418358 | solution.py:67
  38.5 18.1 %while.77 = (s32[]{:T(128)}, f32[6,256]{1,0:T(8,128)S(1)}, f32[7,8192]{1,0:T(8,128)}, f32[6,256]{1,0:T(8,128)S(1)}, s32[]{:T(128)}, /*index=5*/s32[]{:T(128)}, s...) while((s32[]{:T(128)}, f32[6,256]{1,0:T(8,128)S(1)}, ...), condition=%wide.region_10.9_spmd.clone, body=%wide.region_3.8_spmd.clone.sunk | while | flops 42993164 | bytes 399649 | solution.py:58
  40.2 7.2 %fusion.50 = (f32[256]{0:T(256)S(1)}, f32[256]{0:T(256)S(1)}, f32[256]{0:T(256)S(1)}, f32[256]{0:T(256)S(1)}, f32[256]{0:T(256)S(1)}, /*index=5*/f32[256]{0:T(256)S(1)}) fusion(f32[256]{0:T(256)S(1)} %bitcast.131, f32[4096]{0:T(1024)S(1)} %bitcast.123, f32[256]{0:T(256)S(1)} %bitcast.133, f32[4096]{0:T(1024)S(1)} %bitcast.119, f32[256]{0:T(256)S(1)} %bitcast.134, ...), kind=kLoop, calls=%fused_computation.22.clone.1 | loop fusion | flops 42990080 | bytes 126976 | tf_op jit(solution)/shard_map/while/body/eval_jaxpr/while/body/while/body/eval_jaxpr/reduce_sum | solution.py:45
  49.3 7.2 %fusion.50 = (f32[256]{0:T(256)S(1)}, f32[256]{0:T(256)S(1)}, f32[256]{0:T(256)S(1)}, f32[256]{0:T(256)S(1)}, f32[256]{0:T(256)S(1)}, /*index=5*/f32[256]{0:T(256)S(1)}) fusion(f32[256]{0:T(256)S(1)} %bitcast.131, f32[4096]{0:T(1024)S(1)} %bitcast.123, f32[256]{0:T(256)S(1)} %bitcast.133, f32[4096]{0:T(1024)S(1)} %bitcast.119, f32[256]{0:T(256)S(1)} %bitcast.134, ...), kind=kLoop, calls=%fused_computation.22.clone.1 | loop fusion | flops 42990080 | bytes 126976 | tf_op jit(solution)/shard_map/while/body/eval_jaxpr/while/body/while/body/eval_jaxpr/reduce_sum | solution.py:45
  57.3 4.0 %collective-permute-start = (f32[7,8192]{1,0:T(8,128)}, f32[7,8192]{1,0:T(8,128)S(1)}, u32[]{:S(2)}, u32[]{:S(2)}) collective-permute-start(f32[7,8192]{1,0:T(8,128)} %copy.69), channel_id=1, source_target_pairs={{0,8},{8,16},{16,24},{24,32},{32,40},{40,48},{48,56},{56,64},{64,7... | collective-permute-start | bytes 688136 | tf_op jit(solution)/shard_map/while/body/eval_jaxpr/ppermute | solution.py:13
  61.3 18.1 %while.75 = (s32[]{:T(128)}, f32[6,256]{1,0:T(8,128)S(1)}, s32[]{:T(128)}, f32[7,8192]{1,0:T(8,128)}, f32[6,256]{1,0:T(8,128)S(1)}, /*index=5*/s32[]{:T(128)}, s...) while((s32[]{:T(128)}, f32[6,256]{1,0:T(8,128)S(1)}, ...), condition=%wide.region_11.11_spmd, body=%wide.region_2.10_spmd.sunk | while | flops 42994700 | bytes 418358 | solution.py:67
  61.3 18.1 %while.77 = (s32[]{:T(128)}, f32[6,256]{1,0:T(8,128)S(1)}, f32[7,8192]{1,0:T(8,128)}, f32[6,256]{1,0:T(8,128)S(1)}, s32[]{:T(128)}, /*index=5*/s32[]{:T(128)}, s...) while((s32[]{:T(128)}, f32[6,256]{1,0:T(8,128)S(1)}, ...), condition=%wide.region_10.9_spmd.clone, body=%wide.region_3.8_spmd.clone.sunk | while | flops 42993164 | bytes 399649 | solution.py:58
  63.0 7.2 %fusion.50 = (f32[256]{0:T(256)S(1)}, f32[256]{0:T(256)S(1)}, f32[256]{0:T(256)S(1)}, f32[256]{0:T(256)S(1)}, f32[256]{0:T(256)S(1)}, /*index=5*/f32[256]{0:T(256)S(1)}) fusion(f32[256]{0:T(256)S(1)} %bitcast.131, f32[4096]{0:T(1024)S(1)} %bitcast.123, f32[256]{0:T(256)S(1)} %bitcast.133, f32[4096]{0:T(1024)S(1)} %bitcast.119, f32[256]{0:T(256)S(1)} %bitcast.134, ...), kind=kLoop, calls=%fused_computation.22.clone.1 | loop fusion | flops 42990080 | bytes 126976 | tf_op jit(solution)/shard_map/while/body/eval_jaxpr/while/body/while/body/eval_jaxpr/reduce_sum | solution.py:45
  72.2 7.2 %fusion.50 = (f32[256]{0:T(256)S(1)}, f32[256]{0:T(256)S(1)}, f32[256]{0:T(256)S(1)}, f32[256]{0:T(256)S(1)}, f32[256]{0:T(256)S(1)}, /*index=5*/f32[256]{0:T(256)S(1)}) fusion(f32[256]{0:T(256)S(1)} %bitcast.131, f32[4096]{0:T(1024)S(1)} %bitcast.123, f32[256]{0:T(256)S(1)} %bitcast.133, f32[4096]{0:T(1024)S(1)} %bitcast.119, f32[256]{0:T(256)S(1)} %bitcast.134, ...), kind=kLoop, calls=%fused_computation.22.clone.1 | loop fusion | flops 42990080 | bytes 126976 | tf_op jit(solution)/shard_map/while/body/eval_jaxpr/while/body/while/body/eval_jaxpr/reduce_sum | solution.py:45
  80.1 4.0 %collective-permute-start = (f32[7,8192]{1,0:T(8,128)}, f32[7,8192]{1,0:T(8,128)S(1)}, u32[]{:S(2)}, u32[]{:S(2)}) collective-permute-start(f32[7,8192]{1,0:T(8,128)} %copy.69), channel_id=1, source_target_pairs={{0,8},{8,16},{16,24},{24,32},{32,40},{40,48},{48,56},{56,64},{64,7... | collective-permute-start | bytes 688136 | tf_op jit(solution)/shard_map/while/body/eval_jaxpr/ppermute | solution.py:13
  84.1 18.1 %while.75 = (s32[]{:T(128)}, f32[6,256]{1,0:T(8,128)S(1)}, s32[]{:T(128)}, f32[7,8192]{1,0:T(8,128)}, f32[6,256]{1,0:T(8,128)S(1)}, /*index=5*/s32[]{:T(128)}, s...) while((s32[]{:T(128)}, f32[6,256]{1,0:T(8,128)S(1)}, ...), condition=%wide.region_11.11_spmd, body=%wide.region_2.10_spmd.sunk | while | flops 42994700 | bytes 418358 | solution.py:67
  84.2 18.1 %while.77 = (s32[]{:T(128)}, f32[6,256]{1,0:T(8,128)S(1)}, f32[7,8192]{1,0:T(8,128)}, f32[6,256]{1,0:T(8,128)S(1)}, s32[]{:T(128)}, /*index=5*/s32[]{:T(128)}, s...) while((s32[]{:T(128)}, f32[6,256]{1,0:T(8,128)S(1)}, ...), condition=%wide.region_10.9_spmd.clone, body=%wide.region_3.8_spmd.clone.sunk | while | flops 42993164 | bytes 399649 | solution.py:58
  85.9 7.2 %fusion.50 = (f32[256]{0:T(256)S(1)}, f32[256]{0:T(256)S(1)}, f32[256]{0:T(256)S(1)}, f32[256]{0:T(256)S(1)}, f32[256]{0:T(256)S(1)}, /*index=5*/f32[256]{0:T(256)S(1)}) fusion(f32[256]{0:T(256)S(1)} %bitcast.131, f32[4096]{0:T(1024)S(1)} %bitcast.123, f32[256]{0:T(256)S(1)} %bitcast.133, f32[4096]{0:T(1024)S(1)} %bitcast.119, f32[256]{0:T(256)S(1)} %bitcast.134, ...), kind=kLoop, calls=%fused_computation.22.clone.1 | loop fusion | flops 42990080 | bytes 126976 | tf_op jit(solution)/shard_map/while/body/eval_jaxpr/while/body/while/body/eval_jaxpr/reduce_sum | solution.py:45
  95.0 7.2 %fusion.50 = (f32[256]{0:T(256)S(1)}, f32[256]{0:T(256)S(1)}, f32[256]{0:T(256)S(1)}, f32[256]{0:T(256)S(1)}, f32[256]{0:T(256)S(1)}, /*index=5*/f32[256]{0:T(256)S(1)}) fusion(f32[256]{0:T(256)S(1)} %bitcast.131, f32[4096]{0:T(1024)S(1)} %bitcast.123, f32[256]{0:T(256)S(1)} %bitcast.133, f32[4096]{0:T(1024)S(1)} %bitcast.119, f32[256]{0:T(256)S(1)} %bitcast.134, ...), kind=kLoop, calls=%fused_computation.22.clone.1 | loop fusion | flops 42990080 | bytes 126976 | tf_op jit(solution)/shard_map/while/body/eval_jaxpr/while/body/while/body/eval_jaxpr/reduce_sum | solution.py:45
  103.0 5.2 %collective-permute-start = (f32[7,8192]{1,0:T(8,128)}, f32[7,8192]{1,0:T(8,128)S(1)}, u32[]{:S(2)}, u32[]{:S(2)}) collective-permute-start(f32[7,8192]{1,0:T(8,128)} %copy.69), channel_id=1, source_target_pairs={{0,8},{8,16},{16,24},{24,32},{32,40},{40,48},{48,56},{56,64},{64,7... | collective-permute-start | bytes 688136 | tf_op jit(solution)/shard_map/while/body/eval_jaxpr/ppermute | solution.py:13
  108.2 18.1 %while.75 = (s32[]{:T(128)}, f32[6,256]{1,0:T(8,128)S(1)}, s32[]{:T(128)}, f32[7,8192]{1,0:T(8,128)}, f32[6,256]{1,0:T(8,128)S(1)}, /*index=5*/s32[]{:T(128)}, s...) while((s32[]{:T(128)}, f32[6,256]{1,0:T(8,128)S(1)}, ...), condition=%wide.region_11.11_spmd, body=%wide.region_2.10_spmd.sunk | while | flops 42994700 | bytes 418358 | solution.py:67
  108.2 18.1 %while.77 = (s32[]{:T(128)}, f32[6,256]{1,0:T(8,128)S(1)}, f32[7,8192]{1,0:T(8,128)}, f32[6,256]{1,0:T(8,128)S(1)}, s32[]{:T(128)}, /*index=5*/s32[]{:T(128)}, s...) while((s32[]{:T(128)}, f32[6,256]{1,0:T(8,128)S(1)}, ...), condition=%wide.region_10.9_spmd.clone, body=%wide.region_3.8_spmd.clone.sunk | while | flops 42993164 | bytes 399649 | solution.py:58
  109.9 7.2 %fusion.50 = (f32[256]{0:T(256)S(1)}, f32[256]{0:T(256)S(1)}, f32[256]{0:T(256)S(1)}, f32[256]{0:T(256)S(1)}, f32[256]{0:T(256)S(1)}, /*index=5*/f32[256]{0:T(256)S(1)}) fusion(f32[256]{0:T(256)S(1)} %bitcast.131, f32[4096]{0:T(1024)S(1)} %bitcast.123, f32[256]{0:T(256)S(1)} %bitcast.133, f32[4096]{0:T(1024)S(1)} %bitcast.119, f32[256]{0:T(256)S(1)} %bitcast.134, ...), kind=kLoop, calls=%fused_computation.22.clone.1 | loop fusion | flops 42990080 | bytes 126976 | tf_op jit(solution)/shard_map/while/body/eval_jaxpr/while/body/while/body/eval_jaxpr/reduce_sum | solution.py:45
  119.1 7.2 %fusion.50 = (f32[256]{0:T(256)S(1)}, f32[256]{0:T(256)S(1)}, f32[256]{0:T(256)S(1)}, f32[256]{0:T(256)S(1)}, f32[256]{0:T(256)S(1)}, /*index=5*/f32[256]{0:T(256)S(1)}) fusion(f32[256]{0:T(256)S(1)} %bitcast.131, f32[4096]{0:T(1024)S(1)} %bitcast.123, f32[256]{0:T(256)S(1)} %bitcast.133, f32[4096]{0:T(1024)S(1)} %bitcast.119, f32[256]{0:T(256)S(1)} %bitcast.134, ...), kind=kLoop, calls=%fused_computation.22.clone.1 | loop fusion | flops 42990080 | bytes 126976 | tf_op jit(solution)/shard_map/while/body/eval_jaxpr/while/body/while/body/eval_jaxpr/reduce_sum | solution.py:45
  127.0 3.1 %collective-permute-start = (f32[7,8192]{1,0:T(8,128)}, f32[7,8192]{1,0:T(8,128)S(1)}, u32[]{:S(2)}, u32[]{:S(2)}) collective-permute-start(f32[7,8192]{1,0:T(8,128)} %copy.69), channel_id=1, source_target_pairs={{0,8},{8,16},{16,24},{24,32},{32,40},{40,48},{48,56},{56,64},{64,7... | collective-permute-start | bytes 688136 | tf_op jit(solution)/shard_map/while/body/eval_jaxpr/ppermute | solution.py:13
  130.1 18.1 %while.75 = (s32[]{:T(128)}, f32[6,256]{1,0:T(8,128)S(1)}, s32[]{:T(128)}, f32[7,8192]{1,0:T(8,128)}, f32[6,256]{1,0:T(8,128)S(1)}, /*index=5*/s32[]{:T(128)}, s...) while((s32[]{:T(128)}, f32[6,256]{1,0:T(8,128)S(1)}, ...), condition=%wide.region_11.11_spmd, body=%wide.region_2.10_spmd.sunk | while | flops 42994700 | bytes 418358 | solution.py:67
  130.1 18.1 %while.77 = (s32[]{:T(128)}, f32[6,256]{1,0:T(8,128)S(1)}, f32[7,8192]{1,0:T(8,128)}, f32[6,256]{1,0:T(8,128)S(1)}, s32[]{:T(128)}, /*index=5*/s32[]{:T(128)}, s...) while((s32[]{:T(128)}, f32[6,256]{1,0:T(8,128)S(1)}, ...), condition=%wide.region_10.9_spmd.clone, body=%wide.region_3.8_spmd.clone.sunk | while | flops 42993164 | bytes 399649 | solution.py:58
  131.9 7.2 %fusion.50 = (f32[256]{0:T(256)S(1)}, f32[256]{0:T(256)S(1)}, f32[256]{0:T(256)S(1)}, f32[256]{0:T(256)S(1)}, f32[256]{0:T(256)S(1)}, /*index=5*/f32[256]{0:T(256)S(1)}) fusion(f32[256]{0:T(256)S(1)} %bitcast.131, f32[4096]{0:T(1024)S(1)} %bitcast.123, f32[256]{0:T(256)S(1)} %bitcast.133, f32[4096]{0:T(1024)S(1)} %bitcast.119, f32[256]{0:T(256)S(1)} %bitcast.134, ...), kind=kLoop, calls=%fused_computation.22.clone.1 | loop fusion | flops 42990080 | bytes 126976 | tf_op jit(solution)/shard_map/while/body/eval_jaxpr/while/body/while/body/eval_jaxpr/reduce_sum | solution.py:45
  141.0 7.2 %fusion.50 = (f32[256]{0:T(256)S(1)}, f32[256]{0:T(256)S(1)}, f32[256]{0:T(256)S(1)}, f32[256]{0:T(256)S(1)}, f32[256]{0:T(256)S(1)}, /*index=5*/f32[256]{0:T(256)S(1)}) fusion(f32[256]{0:T(256)S(1)} %bitcast.131, f32[4096]{0:T(1024)S(1)} %bitcast.123, f32[256]{0:T(256)S(1)} %bitcast.133, f32[4096]{0:T(1024)S(1)} %bitcast.119, f32[256]{0:T(256)S(1)} %bitcast.134, ...), kind=kLoop, calls=%fused_computation.22.clone.1 | loop fusion | flops 42990080 | bytes 126976 | tf_op jit(solution)/shard_map/while/body/eval_jaxpr/while/body/while/body/eval_jaxpr/reduce_sum | solution.py:45
  149.0 3.1 %collective-permute-start = (f32[7,8192]{1,0:T(8,128)}, f32[7,8192]{1,0:T(8,128)S(1)}, u32[]{:S(2)}, u32[]{:S(2)}) collective-permute-start(f32[7,8192]{1,0:T(8,128)} %copy.69), channel_id=1, source_target_pairs={{0,8},{8,16},{16,24},{24,32},{32,40},{40,48},{48,56},{56,64},{64,7... | collective-permute-start | bytes 688136 | tf_op jit(solution)/shard_map/while/body/eval_jaxpr/ppermute | solution.py:13
  152.1 18.1 %while.75 = (s32[]{:T(128)}, f32[6,256]{1,0:T(8,128)S(1)}, s32[]{:T(128)}, f32[7,8192]{1,0:T(8,128)}, f32[6,256]{1,0:T(8,128)S(1)}, /*index=5*/s32[]{:T(128)}, s...) while((s32[]{:T(128)}, f32[6,256]{1,0:T(8,128)S(1)}, ...), condition=%wide.region_11.11_spmd, body=%wide.region_2.10_spmd.sunk | while | flops 42994700 | bytes 418358 | solution.py:67
  152.1 18.1 %while.77 = (s32[]{:T(128)}, f32[6,256]{1,0:T(8,128)S(1)}, f32[7,8192]{1,0:T(8,128)}, f32[6,256]{1,0:T(8,128)S(1)}, s32[]{:T(128)}, /*index=5*/s32[]{:T(128)}, s...) while((s32[]{:T(128)}, f32[6,256]{1,0:T(8,128)S(1)}, ...), condition=%wide.region_10.9_spmd.clone, body=%wide.region_3.8_spmd.clone.sunk | while | flops 42993164 | bytes 399649 | solution.py:58
  153.8 7.2 %fusion.50 = (f32[256]{0:T(256)S(1)}, f32[256]{0:T(256)S(1)}, f32[256]{0:T(256)S(1)}, f32[256]{0:T(256)S(1)}, f32[256]{0:T(256)S(1)}, /*index=5*/f32[256]{0:T(256)S(1)}) fusion(f32[256]{0:T(256)S(1)} %bitcast.131, f32[4096]{0:T(1024)S(1)} %bitcast.123, f32[256]{0:T(256)S(1)} %bitcast.133, f32[4096]{0:T(1024)S(1)} %bitcast.119, f32[256]{0:T(256)S(1)} %bitcast.134, ...), kind=kLoop, calls=%fused_computation.22.clone.1 | loop fusion | flops 42990080 | bytes 126976 | tf_op jit(solution)/shard_map/while/body/eval_jaxpr/while/body/while/body/eval_jaxpr/reduce_sum | solution.py:45
  162.9 7.2 %fusion.50 = (f32[256]{0:T(256)S(1)}, f32[256]{0:T(256)S(1)}, f32[256]{0:T(256)S(1)}, f32[256]{0:T(256)S(1)}, f32[256]{0:T(256)S(1)}, /*index=5*/f32[256]{0:T(256)S(1)}) fusion(f32[256]{0:T(256)S(1)} %bitcast.131, f32[4096]{0:T(1024)S(1)} %bitcast.123, f32[256]{0:T(256)S(1)} %bitcast.133, f32[4096]{0:T(1024)S(1)} %bitcast.119, f32[256]{0:T(256)S(1)} %bitcast.134, ...), kind=kLoop, calls=%fused_computation.22.clone.1 | loop fusion | flops 42990080 | bytes 126976 | tf_op jit(solution)/shard_map/while/body/eval_jaxpr/while/body/while/body/eval_jaxpr/reduce_sum | solution.py:45
  170.9 3.1 %collective-permute-start = (f32[7,8192]{1,0:T(8,128)}, f32[7,8192]{1,0:T(8,128)S(1)}, u32[]{:S(2)}, u32[]{:S(2)}) collective-permute-start(f32[7,8192]{1,0:T(8,128)} %copy.69), channel_id=1, source_target_pairs={{0,8},{8,16},{16,24},{24,32},{32,40},{40,48},{48,56},{56,64},{64,7... | collective-permute-start | bytes 688136 | tf_op jit(solution)/shard_map/while/body/eval_jaxpr/ppermute | solution.py:13
  174.0 18.1 %while.75 = (s32[]{:T(128)}, f32[6,256]{1,0:T(8,128)S(1)}, s32[]{:T(128)}, f32[7,8192]{1,0:T(8,128)}, f32[6,256]{1,0:T(8,128)S(1)}, /*index=5*/s32[]{:T(128)}, s...) while((s32[]{:T(128)}, f32[6,256]{1,0:T(8,128)S(1)}, ...), condition=%wide.region_11.11_spmd, body=%wide.region_2.10_spmd.sunk | while | flops 42994700 | bytes 418358 | solution.py:67
  174.0 18.1 %while.77 = (s32[]{:T(128)}, f32[6,256]{1,0:T(8,128)S(1)}, f32[7,8192]{1,0:T(8,128)}, f32[6,256]{1,0:T(8,128)S(1)}, s32[]{:T(128)}, /*index=5*/s32[]{:T(128)}, s...) while((s32[]{:T(128)}, f32[6,256]{1,0:T(8,128)S(1)}, ...), condition=%wide.region_10.9_spmd.clone, body=%wide.region_3.8_spmd.clone.sunk | while | flops 42993164 | bytes 399649 | solution.py:58
  175.7 7.2 %fusion.50 = (f32[256]{0:T(256)S(1)}, f32[256]{0:T(256)S(1)}, f32[256]{0:T(256)S(1)}, f32[256]{0:T(256)S(1)}, f32[256]{0:T(256)S(1)}, /*index=5*/f32[256]{0:T(256)S(1)}) fusion(f32[256]{0:T(256)S(1)} %bitcast.131, f32[4096]{0:T(1024)S(1)} %bitcast.123, f32[256]{0:T(256)S(1)} %bitcast.133, f32[4096]{0:T(1024)S(1)} %bitcast.119, f32[256]{0:T(256)S(1)} %bitcast.134, ...), kind=kLoop, calls=%fused_computation.22.clone.1 | loop fusion | flops 42990080 | bytes 126976 | tf_op jit(solution)/shard_map/while/body/eval_jaxpr/while/body/while/body/eval_jaxpr/reduce_sum | solution.py:45
  184.9 7.2 %fusion.50 = (f32[256]{0:T(256)S(1)}, f32[256]{0:T(256)S(1)}, f32[256]{0:T(256)S(1)}, f32[256]{0:T(256)S(1)}, f32[256]{0:T(256)S(1)}, /*index=5*/f32[256]{0:T(256)S(1)}) fusion(f32[256]{0:T(256)S(1)} %bitcast.131, f32[4096]{0:T(1024)S(1)} %bitcast.123, f32[256]{0:T(256)S(1)} %bitcast.133, f32[4096]{0:T(1024)S(1)} %bitcast.119, f32[256]{0:T(256)S(1)} %bitcast.134, ...), kind=kLoop, calls=%fused_computation.22.clone.1 | loop fusion | flops 42990080 | bytes 126976 | tf_op jit(solution)/shard_map/while/body/eval_jaxpr/while/body/while/body/eval_jaxpr/reduce_sum | solution.py:45
  192.1 15.1 %while.74 = (s32[]{:T(128)}, f32[6,256]{1,0:T(8,128)S(1)}, s32[]{:T(128)}, f32[7,8192]{1,0:T(8,128)S(1)}, f32[6,256]{1,0:T(8,128)S(1)}, /*index=5*/s32[]{:T(128)...) while((s32[]{:T(128)}, f32[6,256]{1,0:T(8,128)S(1)}, ...), condition=%wide.region_22.23_spmd, body=%wide.region_13.22_spmd.sunk | while | flops 42994700 | bytes 418358 | solution.py:67
  192.2 15.0 %while.76 = (s32[]{:T(128)}, f32[6,256]{1,0:T(8,128)S(1)}, f32[7,8192]{1,0:T(8,128)S(1)}, f32[6,256]{1,0:T(8,128)S(1)}, s32[]{:T(128)}, /*index=5*/s32[]{:T(128)...) while((s32[]{:T(128)}, f32[6,256]{1,0:T(8,128)S(1)}, ...), condition=%wide.region_21.21_spmd.clone, body=%wide.region_14.20_spmd.clone.sunk | while | flops 42993164 | bytes 399649 | solution.py:58
  192.5 7.2 %fusion.47 = (f32[256]{0:T(256)S(1)}, f32[256]{0:T(256)S(1)}, f32[256]{0:T(256)S(1)}, f32[256]{0:T(256)S(1)}, f32[256]{0:T(256)S(1)}, /*index=5*/f32[256]{0:T(256)S(1)}) fusion(f32[256]{0:T(256)S(1)} %bitcast.150, f32[4096]{0:T(1024)S(1)} %bitcast.142, f32[256]{0:T(256)S(1)} %bitcast.152, f32[4096]{0:T(1024)S(1)} %bitcast.138, f32[256]{0:T(256)S(1)} %bitcast.153, ...), kind=kLoop, calls=%fused_computation.57.clone.1 | loop fusion | flops 42990080 | bytes 126976 | tf_op jit(solution)/shard_map/while/body/while/body/eval_jaxpr/reduce_sum | solution.py:45
  200.0 7.2 %fusion.47 = (f32[256]{0:T(256)S(1)}, f32[256]{0:T(256)S(1)}, f32[256]{0:T(256)S(1)}, f32[256]{0:T(256)S(1)}, f32[256]{0:T(256)S(1)}, /*index=5*/f32[256]{0:T(256)S(1)}) fusion(f32[256]{0:T(256)S(1)} %bitcast.150, f32[4096]{0:T(1024)S(1)} %bitcast.142, f32[256]{0:T(256)S(1)} %bitcast.152, f32[4096]{0:T(1024)S(1)} %bitcast.138, f32[256]{0:T(256)S(1)} %bitcast.153, ...), kind=kLoop, calls=%fused_computation.57.clone.1 | loop fusion | flops 42990080 | bytes 126976 | tf_op jit(solution)/shard_map/while/body/while/body/eval_jaxpr/reduce_sum | solution.py:45
  207.2 19.8 %psum.7 = f32[6,256]{1,0:T(8,128)S(1)} all-reduce(f32[6,256]{1,0:T(8,128)S(1)} %get-tuple-element.361), channel_id=1, replica_groups=mesh['blk'=64,'rep'=8] {'rep'}, use_global_device_ids=true, to_apply=%region_23.24 | all-reduce | flops 1536 | bytes 12288 | tf_op jit(solution)/shard_map/psum | solution.py:92
  (114 shorter events, 37.6 us)
Async XLA Ops:
  0.6 12.8 %copy-start = (f32[8192]{0:T(1024)S(1)}, f32[8192]{0:T(1024)}, u32[]{:S(2)}) copy-start(f32[8192]{0:T(1024)} %param.21) | copy-start | bytes 98308
  0.6 16.9 %copy-start.1 = (s32[256]{0:T(256)S(1)}, s32[256]{0:T(256)}, u32[]{:S(2)}) copy-start(s32[256]{0:T(256)} %param.23) | copy-start | bytes 3076
  3.5 10.0 %collective-permute-start.1 = (f32[7,8192]{1,0:T(8,128)S(1)}, f32[7,8192]{1,0:T(8,128)S(1)}, u32[]{:S(2)}, u32[]{:S(2)}) collective-permute-start(f32[7,8192]{1,0:T(8,128)S(1)} %pad_maximum_fusion), channel_id=1, source_target_pairs={{0,64},{8,72},{16,80},{24,88},{32,96},{40,104},{48,112},{56,120},{... | collective-permute-start | bytes 688136 | tf_op jit(solution)/shard_map/ppermute | solution.py:13
  13.6 9.3 %collective-permute-start.2 = (f32[7,8192]{1,0:T(8,128)S(1)}, f32[7,8192]{1,0:T(8,128)S(1)}, u32[]{:S(2)}, u32[]{:S(2)}) collective-permute-start(f32[7,8192]{1,0:T(8,128)S(1)} %broadcast_select_fusion), channel_id=1, source_target_pairs={{0,128},{8,136},{16,144},{24,152},{32,160},{40,168},{48,176},{56,1... | collective-permute-start | bytes 688136 | tf_op jit(solution)/shard_map/ppermute | solution.py:13
  22.9 8.7 %collective-permute-start.3 = (f32[7,8192]{1,0:T(8,128)S(1)}, f32[7,8192]{1,0:T(8,128)S(1)}, u32[]{:S(2)}, u32[]{:S(2)}) collective-permute-start(f32[7,8192]{1,0:T(8,128)S(1)} %broadcast_select_fusion.1), channel_id=1, source_target_pairs={{0,256},{8,264},{16,272},{24,280},{32,288},{40,296},{48,304},{56,3... | collective-permute-start | bytes 688136 | tf_op jit(solution)/shard_map/ppermute | solution.py:13
  32.3 24.2 %collective-permute-start = (f32[7,8192]{1,0:T(8,128)}, f32[7,8192]{1,0:T(8,128)S(1)}, u32[]{:S(2)}, u32[]{:S(2)}) collective-permute-start(f32[7,8192]{1,0:T(8,128)} %copy.69), channel_id=1, source_target_pairs={{0,8},{8,16},{16,24},{24,32},{32,40},{40,48},{48,56},{56,64},{64,7... | collective-permute-start | bytes 688136 | tf_op jit(solution)/shard_map/while/body/eval_jaxpr/ppermute | solution.py:13
  57.3 22.1 %collective-permute-start = (f32[7,8192]{1,0:T(8,128)}, f32[7,8192]{1,0:T(8,128)S(1)}, u32[]{:S(2)}, u32[]{:S(2)}) collective-permute-start(f32[7,8192]{1,0:T(8,128)} %copy.69), channel_id=1, source_target_pairs={{0,8},{8,16},{16,24},{24,32},{32,40},{40,48},{48,56},{56,64},{64,7... | collective-permute-start | bytes 688136 | tf_op jit(solution)/shard_map/while/body/eval_jaxpr/ppermute | solution.py:13
  80.1 22.1 %collective-permute-start = (f32[7,8192]{1,0:T(8,128)}, f32[7,8192]{1,0:T(8,128)S(1)}, u32[]{:S(2)}, u32[]{:S(2)}) collective-permute-start(f32[7,8192]{1,0:T(8,128)} %copy.69), channel_id=1, source_target_pairs={{0,8},{8,16},{16,24},{24,32},{32,40},{40,48},{48,56},{56,64},{64,7... | collective-permute-start | bytes 688136 | tf_op jit(solution)/shard_map/while/body/eval_jaxpr/ppermute | solution.py:13
  103.0 23.3 %collective-permute-start = (f32[7,8192]{1,0:T(8,128)}, f32[7,8192]{1,0:T(8,128)S(1)}, u32[]{:S(2)}, u32[]{:S(2)}) collective-permute-start(f32[7,8192]{1,0:T(8,128)} %copy.69), channel_id=1, source_target_pairs={{0,8},{8,16},{16,24},{24,32},{32,40},{40,48},{48,56},{56,64},{64,7... | collective-permute-start | bytes 688136 | tf_op jit(solution)/shard_map/while/body/eval_jaxpr/ppermute | solution.py:13
  127.0 21.2 %collective-permute-start = (f32[7,8192]{1,0:T(8,128)}, f32[7,8192]{1,0:T(8,128)S(1)}, u32[]{:S(2)}, u32[]{:S(2)}) collective-permute-start(f32[7,8192]{1,0:T(8,128)} %copy.69), channel_id=1, source_target_pairs={{0,8},{8,16},{16,24},{24,32},{32,40},{40,48},{48,56},{56,64},{64,7... | collective-permute-start | bytes 688136 | tf_op jit(solution)/shard_map/while/body/eval_jaxpr/ppermute | solution.py:13
  149.0 21.2 %collective-permute-start = (f32[7,8192]{1,0:T(8,128)}, f32[7,8192]{1,0:T(8,128)S(1)}, u32[]{:S(2)}, u32[]{:S(2)}) collective-permute-start(f32[7,8192]{1,0:T(8,128)} %copy.69), channel_id=1, source_target_pairs={{0,8},{8,16},{16,24},{24,32},{32,40},{40,48},{48,56},{56,64},{64,7... | collective-permute-start | bytes 688136 | tf_op jit(solution)/shard_map/while/body/eval_jaxpr/ppermute | solution.py:13
  170.9 21.2 %collective-permute-start = (f32[7,8192]{1,0:T(8,128)}, f32[7,8192]{1,0:T(8,128)S(1)}, u32[]{:S(2)}, u32[]{:S(2)}) collective-permute-start(f32[7,8192]{1,0:T(8,128)} %copy.69), channel_id=1, source_target_pairs={{0,8},{8,16},{16,24},{24,32},{32,40},{40,48},{48,56},{56,64},{64,7... | collective-permute-start | bytes 688136 | tf_op jit(solution)/shard_map/while/body/eval_jaxpr/ppermute | solution.py:13
where the time goes:
time: 229 us; the launch traced here: 228 us
  other arithmetic  119 us (52%)
  starting transfers between devices  41 us (18%)
  local copies, waits for them, and re-layouts  37.2 us (16%)
  blocking collectives  19.8 us (9%)
  waiting for transfers between devices  7.61 us (3%)
    reduce_sum x16, other arithmetic, pair_sums(): jnp.sum(strength * (drift_three - radial * delta_three), axis=1)  115 us
    ppermute x10, starting transfers between devices, shifted(): lax.ppermute(value, axis, [(i, (i + by) % size) for i in range(size)])  41 us
    slice x32, local copies, waits for them, and re-layouts, pair_sums(): drift_one = sources[3][None, :] - targets[3][:, None]  25.7 us
    psum x1, blocking collectives, replica_total(): return lax.psum(sums, 'rep')  19.8 us
    ppermute x10, waiting for transfers between devices, shifted(): lax.ppermute(value, axis, [(i, (i + by) % size) for i in range(size)])  7.61 us
    another operation x8, local copies, waits for them, and re-layouts  4.85 us
  transfers between devices with their start and end apart: 10, of which 3 were waited for; matrix products, arithmetic and copies ran while one was open for 58% of the time, Pallas kernels for 0%

commit v1 on v0

v1 whole, which is shorter than its diff:
```python
import functools

import jax
import jax.numpy as jnp
from jax import lax
from jax.experimental import pallas as pl
from jax.experimental.pallas import tpu as pltpu
from jax.sharding import PartitionSpec as P

SOFTENING = 0.001
MESH = pl.DeviceIdType.MESH
F32 = jnp.float32
BF16 = jnp.bfloat16
TEAMS = 64
REPS = 8
CAP = 256
SHARE = CAP // REPS
STARS_DEV = 8192
MAX_ROWS = TEAMS * SHARE
TB = 64
CHUNK = 1024


def iota(shape, dim):
    return lax.broadcasted_iota(jnp.int32, shape, dim)


def phase_of(team, rep):
    return lax.rem(rep + 3 * team, REPS)


def split3(x):
    a = x.astype(BF16)
    rest = x - a.astype(F32)
    b = rest.astype(BF16)
    c = (rest - b.astype(F32)).astype(BF16)
    return a, b, c


def fanned(rows, unit):
    sub = lax.rem(iota((8, 128), 0), 4)
    out = rows
    for k in range(1, 4):
        out = jnp.where(sub == k, pltpu.roll(rows, unit * k % 128, 1), out)
    return out


def signal_peers(barrier, axis, me, size):
    def one(step, carry):
        pl.semaphore_signal(
            barrier, inc=1, device_id={axis: lax.rem(me + step, size)}, device_id_type=MESH
        )
        return carry

    lax.fori_loop(1, size, one, 0)


def predict_kernel(index_ref, pos, vel, acc, jrk, mass, elapsed, own, field):
    team = lax.axis_index("blk")
    rep = lax.axis_index("rep")
    h = elapsed[...]
    v, a, j = vel[...], acc[...], jrk[...]
    field[0:3, :] = pos[...] + h * (v + h * (0.5 * a + h / 6.0 * j))
    field[3:6, :] = v + h * (a + 0.5 * h * j)
    field[6:7, :] = jnp.ones((1, STARS_DEV), F32)
    field[7:8, :] = jnp.zeros((1, STARS_DEV), F32)

    phase = phase_of(team, rep)
    lane = iota((8, 128), 1)
    sub = iota((8, 128), 0)
    picked = jnp.zeros((8, 128), F32)
    for k in range(SHARE):
        index = index_ref[REPS * k + phase]
        local = jnp.clip(index - team * STARS_DEV, 0, STARS_DEV - 1)
        tile = field[:, pl.ds(pl.multiple_of(lax.div(local, 128) * 128, 128), 128)]
        turned = pltpu.roll(tile, lax.rem(k - lax.rem(local, 128) + 128, 128), 1)
        picked = jnp.where((lane == k) & (index >= 0), turned, picked)
    spread = fanned(picked, 32)
    spread = jnp.where(lane // 32 == lax.rem(sub, 4), spread, 0.0)
    own[...] = jnp.concatenate(
        [jnp.sum(spread[0:4], axis=0, keepdims=True), jnp.sum(spread[4:8], axis=0, keepdims=True)], 0
    )
    field[6:7, :] = mass[...]


def share_kernel(own, targets_out, offset_out, recv, send_sem, recv_sem):
    team = lax.axis_index("blk")
    barrier = pltpu.get_barrier_semaphore()
    signal_peers(barrier, "blk", team, TEAMS)
    recv[team] = own[...]
    pl.semaphore_wait(barrier, TEAMS - 1)

    def send(step, carry):
        pltpu.make_async_remote_copy(
            src_ref=own,
            dst_ref=recv.at[team],
            send_sem=send_sem,
            recv_sem=recv_sem,
            device_id={"blk": lax.rem(team + step, TEAMS)},
            device_id_type=MESH,
        ).start()
        return carry

    lax.fori_loop(1, TEAMS, send, 0)
    pltpu.make_async_copy(recv.at[pl.ds(0, TEAMS - 1)], recv.at[pl.ds(0, TEAMS - 1)], recv_sem).wait()
    pltpu.make_async_copy(recv.at[pl.ds(0, TEAMS - 1)], recv.at[pl.ds(0, TEAMS - 1)], send_sem).wait()
    got = recv[...]
    targets_out[...] = got
    flag_lanes = iota((TEAMS, 128), 1)
    flags = jnp.where((flag_lanes >= 64) & (flag_lanes < 96), got[:, 1, :], 0.0)
    counts = jnp.sum(flags, axis=1, keepdims=True)
    before = jnp.where(iota((TEAMS, 128), 0) < flag_lanes, counts, 0.0)
    offset_out[...] = jnp.sum(before, axis=0, keepdims=True).astype(jnp.int32)


def pair_kernel(offset, targets, field, partial, comp, comp_out, tb, ft, fs, bmat, sum_s, sum_t):
    lane = iota((8, 128), 1)
    sub = iota((8, 128), 0)
    total = offset[0, TEAMS]
    tiles = lax.div(total + 127, 128)

    def clear(tile, carry):
        comp[:, pl.ds(pl.multiple_of(tile * 128, 128), 128)] = jnp.zeros((8, 128), F32)
        return carry

    lax.fori_loop(0, tiles + 2, clear, 0)

    def compact(team, carry):
        start = offset[0, team]
        count = offset[0, team + 1] - start
        message = targets[team]
        rows = jnp.where(sub < 4, message[0:1, :], message[1:2, :])
        rows = fanned(rows, 96)
        rows = jnp.where(lane < count, rows, 0.0)
        shift = lax.rem(start, 128)
        rows = pltpu.roll(rows, shift, 1)
        first = pl.multiple_of(lax.div(start, 128) * 128, 128)
        comp[:, pl.ds(first, 128)] += jnp.where(lane >= shift, rows, 0.0)
        comp[:, pl.ds(first + 128, 128)] += jnp.where(lane < shift, rows, 0.0)
        return carry

    lax.fori_loop(0, TEAMS, compact, 0)

    def target_tile(tile, carry):
        at = pl.multiple_of(tile * 128, 128)
        rows = comp[:, pl.ds(at, 128)]
        for k in range(3):
            tb[k, pl.ds(at, 128), :] = jnp.transpose(jnp.broadcast_to(rows[k : k + 1, :], (128, 128)))
        inner = rows[0:1] * rows[3:4] + rows[1:2] * rows[4:5] + rows[2:3] * rows[5:6]
        y = jnp.concatenate([-rows[3:6], -rows[0:3], jnp.ones((1, 128), F32), inner], 0)
        a, b, c = (part.astype(F32) for part in split3(y))
        stack = jnp.concatenate([a, b, a, b, c, a, jnp.zeros((80, 128), F32)], 0)
        ft[pl.ds(at, 128), :] = jnp.transpose(stack).astype(BF16)
        return carry

    lax.fori_loop(0, tiles, target_tile, 0)

    def source_tile(tile, carry):
        at = pl.multiple_of(tile * 128, 128)
        rows = field[:, pl.ds(at, 128)]
        inner = rows[0:1] * rows[3:4] + rows[1:2] * rows[4:5] + rows[2:3] * rows[5:6]
        x = jnp.concatenate([rows[0:6], inner, jnp.ones((1, 128), F32)], 0)
        a, b, c = (part.astype(F32) for part in split3(x))
        stack = jnp.concatenate([a, a, b, b, a, c, jnp.zeros((80, 128), F32)], 0)
        fs[:, pl.ds(at, 128)] = stack.astype(BF16)
        weighted = jnp.where(sub < 6, rows * rows[6:7, :], rows)
        a, b, c = (part.astype(F32) for part in split3(weighted))
        stack = jnp.concatenate([a, b, c, jnp.zeros((104, 128), F32)], 0)
        bmat[pl.ds(at, 128), :] = jnp.transpose(stack).astype(BF16)
        return carry

    lax.fori_loop(0, STARS_DEV // 128, source_tile, 0)

    def block(number, carry):
        at = pl.multiple_of(number * TB, TB)

        def chunk(step, sums):
            base = pl.multiple_of(step * CHUNK, CHUNK)
            twist = jnp.dot(ft[pl.ds(at, TB), :], fs[:, pl.ds(base, CHUNK)], preferred_element_type=F32)
            left = []
            for k in range(CHUNK // 256):
                parts = [[], [], [], []]
                for g in range(TB // 16):
                    halves = []
                    for m in range(2):
                        cols = pl.ds(base + k * 256 + m * 128, 128)
                        d = [field[c : c + 1, cols] - tb[c, pl.ds(at + g * 16, 16), :] for c in range(3)]
                        r2 = d[0] * d[0] + d[1] * d[1] + d[2] * d[2] + SOFTENING
                        q = lax.rsqrt(r2)
                        q2 = q * q
                        s = q * q2
                        u = twist[g * 16 : g * 16 + 16, k * 256 + m * 128 : k * 256 + m * 128 + 128]
                        t = (u * q2) * s
                        s_hi, t_hi = s.astype(BF16), t.astype(BF16)
                        s_lo = (s - s_hi.astype(F32)).astype(BF16)
                        t_lo = (t - t_hi.astype(F32)).astype(BF16)
                        halves.append((s_hi, t_hi, s_lo, t_lo))
                    for n in range(4):
                        parts[n].append(jnp.concatenate([halves[0][n], halves[1][n]], 1))
                hi = jnp.concatenate(parts[0] + parts[1], 0)
                lo = jnp.concatenate(parts[2] + parts[3], 0)
                left += [hi, lo]
            right = []
            for k in range(CHUNK // 256):
                b = bmat[pl.ds(base + k * 256, 256), :]
                right += [b, b]
            out = jnp.dot(
                jnp.concatenate(left, 1), jnp.concatenate(right, 0), preferred_element_type=F32
            )
            return sums + out

        sums = lax.fori_loop(0, STARS_DEV // CHUNK, chunk, jnp.zeros((2 * TB, 128), F32))
        sum_s[pl.ds(at, TB), :] = sums[:TB]
        sum_t[pl.ds(at, TB), :] = sums[TB:]
        return carry

    lax.fori_loop(0, lax.div(total + TB - 1, TB), block, 0)

    def result_tile(tile, carry):
        at = pl.multiple_of(tile * 128, 128)
        rows = comp[:, pl.ds(at, 128)]

        def folded(ref):
            cols = jnp.transpose(ref[pl.ds(at, 128), :])
            part = cols[0:8] + cols[8:16] + cols[16:24]
            return part - rows * part[6:7, :]

        g_s, g_t = folded(sum_s), folded(sum_t)
        g_t = pltpu.roll(g_t, 3, 0)
        out = jnp.where((sub >= 3) & (sub < 6), g_s - 3.0 * g_t, g_s)
        comp_out[:, pl.ds(at, 128)] = jnp.where(sub < 6, out, 0.0)
        return carry

    lax.fori_loop(0, tiles, result_tile, 0)

    def expand(team, carry):
        start = offset[0, team]
        count = offset[0, team + 1] - start
        shift = lax.rem(start, 128)
        first = pl.multiple_of(lax.div(start, 128) * 128, 128)
        both = jnp.where(lane >= shift, comp_out[:, pl.ds(first, 128)], comp_out[:, pl.ds(first + 128, 128)])
        rows = pltpu.roll(both, lax.rem(128 - shift, 128), 1)
        rows = jnp.where(lane < count, rows, 0.0)
        rows = fanned(rows, 32)
        rows = jnp.where(lane // 32 == lax.rem(sub, 4), rows, 0.0)
        partial[team] = jnp.concatenate(
            [jnp.sum(rows[0:4], axis=0, keepdims=True), jnp.sum(rows[4:8], axis=0, keepdims=True)], 0
        )
        return carry

    lax.fori_loop(0, TEAMS, expand, 0)


def total_kernel(partial, live, force, new_jerk, recv, mine, ring, send_sem, recv_sem, send_sem2, recv_sem2):
    team = lax.axis_index("blk")
    rep = lax.axis_index("rep")
    barrier = pltpu.get_barrier_semaphore()
    signal_peers(barrier, "blk", team, TEAMS)
    signal_peers(barrier, "rep", rep, REPS)
    phase = phase_of(team, rep)
    recv[team] = partial[team]
    source = iota((CAP, CAP), 0)
    slot = iota((CAP, CAP), 1)
    place = jnp.where(slot == lax.rem(source, SHARE) * REPS + source // SHARE, 1.0, 0.0).astype(BF16)
    pl.semaphore_wait(barrier, TEAMS + REPS - 2)

    def send(step, carry):
        peer = lax.rem(team + step, TEAMS)
        pltpu.make_async_remote_copy(
            src_ref=partial.at[peer],
            dst_ref=recv.at[team],
            send_sem=send_sem,
            recv_sem=recv_sem,
            device_id={"blk": peer},
            device_id_type=MESH,
        ).start()
        return carry

    lax.fori_loop(1, TEAMS, send, 0)
    pltpu.make_async_copy(recv.at[pl.ds(0, TEAMS - 1)], recv.at[pl.ds(0, TEAMS - 1)], recv_sem).wait()
    summed = jnp.sum(recv[...], axis=0)
    mine[...] = summed
    ring[phase] = summed

    def pass_on(step, carry):
        pltpu.make_async_remote_copy(
            src_ref=mine,
            dst_ref=ring.at[phase],
            send_sem=send_sem2,
            recv_sem=recv_sem2,
            device_id={"rep": lax.rem(rep + step, REPS)},
            device_id_type=MESH,
        ).start()
        return carry

    lax.fori_loop(1, REPS, pass_on, 0)
    pltpu.make_async_copy(recv.at[pl.ds(0, TEAMS - 1)], recv.at[pl.ds(0, TEAMS - 1)], send_sem).wait()
    pltpu.make_async_copy(ring.at[pl.ds(0, REPS - 1)], ring.at[pl.ds(0, REPS - 1)], recv_sem2).wait()
    pltpu.make_async_copy(ring.at[pl.ds(0, REPS - 1)], ring.at[pl.ds(0, REPS - 1)], send_sem2).wait()
    lane = iota((8, 128), 1)
    sub = iota((8, 128), 0)
    halves = []
    for half in range(2):
        tile = jnp.zeros((8, 128), F32)
        for k in range(4):
            message = ring[half * 4 + k]
            rows = jnp.where(sub < 4, message[0:1, :], message[1:2, :])
            rows = fanned(rows, 96)
            rows = rows if k == 0 else pltpu.roll(rows, 32 * k, 1)
            tile = jnp.where(lane // 32 == k, rows, tile)
        halves.append(tile)
    x = jnp.concatenate(halves, 1)
    a, b, c = (part.astype(F32) for part in split3(x))
    stack = jnp.concatenate([a, b, c, jnp.zeros((8, CAP), F32)], 0).astype(BF16)
    moved = jnp.dot(stack, place, preferred_element_type=F32)
    sums = moved[0:8] + moved[8:16] + moved[16:24]
    scaled = jnp.where(live[...] >= 0, sums / (STARS_DEV * TEAMS), 0.0)
    force[...] = scaled[0:3]
    new_jerk[...] = scaled[3:6]


def in_vmem():
    return pl.BlockSpec(memory_space=pltpu.VMEM)


def in_smem():
    return pl.BlockSpec(memory_space=pltpu.SMEM)


def body(position, velocity, accel, jerk, mass, elapsed, active_index):
    shape = jax.ShapeDtypeStruct
    message = pltpu.VMEM((TEAMS, 2, 128), F32)
    dma = pltpu.SemaphoreType.DMA
    own, field = pl.pallas_call(
        predict_kernel,
        out_shape=(shape((2, 128), F32), shape((8, STARS_DEV), F32)),
        in_specs=[in_smem()] + [in_vmem()] * 6,
        out_specs=(in_vmem(),) * 2,
        name="predict",
    )(active_index, position, velocity, accel, jerk, mass[None, :], elapsed[None, :])
    targets, offset = pl.pallas_call(
        share_kernel,
        out_shape=(shape((TEAMS, 2, 128), F32), shape((1, 128), jnp.int32)),
        in_specs=[in_vmem()],
        out_specs=(in_vmem(),) * 2,
        scratch_shapes=[message, dma, dma],
        compiler_params=pltpu.CompilerParams(collective_id=0, has_side_effects=True),
        name="share",
    )(own)
    partial = pl.pallas_call(
        pair_kernel,
        out_shape=shape((TEAMS, 2, 128), F32),
        in_specs=[in_smem(), in_vmem(), in_vmem()],
        out_specs=in_vmem(),
        scratch_shapes=[
            pltpu.VMEM((8, MAX_ROWS + 256), F32),
            pltpu.VMEM((8, MAX_ROWS + 256), F32),
            pltpu.VMEM((3, MAX_ROWS, 128), F32),
            pltpu.VMEM((MAX_ROWS, 128), BF16),
            pltpu.VMEM((128, STARS_DEV), BF16),
            pltpu.VMEM((STARS_DEV, 128), BF16),
            pltpu.VMEM((MAX_ROWS, 128), F32),
            pltpu.VMEM((MAX_ROWS, 128), F32),
        ],
        compiler_params=pltpu.CompilerParams(vmem_limit_bytes=48 * 2**20),
        name="pairs",
    )(offset, targets, field)
    return pl.pallas_call(
        total_kernel,
        out_shape=(shape((3, CAP), F32), shape((3, CAP), F32)),
        in_specs=[in_vmem(), in_vmem()],
        out_specs=(in_vmem(),) * 2,
        scratch_shapes=[message, pltpu.VMEM((2, 128), F32), pltpu.VMEM((REPS, 2, 128), F32), dma, dma, dma, dma],
        compiler_params=pltpu.CompilerParams(collective_id=1, has_side_effects=True),
        name="totals",
    )(partial, active_index[None, :])


def solution(mesh):
    in_specs = (
        P(None, "blk"),
        P(None, "blk"),
        P(None, "blk"),
        P(None, "blk"),
        P("blk"),
        P("blk"),
        P("blk"),
    )
    out_specs = (P(None, "blk"), P(None, "blk"))
    return jax.shard_map(body, mesh=mesh, in_specs=in_specs, out_specs=out_specs, check_vma=False)
```

time: 229 us -> 107 us (0.47); the launches traced: 228 us -> 109 us
  other arithmetic: 119 us -> 0 us
  Pallas kernels: 0 us -> 103 us
  starting transfers between devices: 41 us -> 0 us
  local copies, waits for them, and re-layouts: 37.2 us -> 4.93 us
  blocking collectives: 19.8 us -> 0 us
  waiting for transfers between devices: 7.61 us -> 0 us
    reduce_sum x17 -> x0, other arithmetic: 116 us -> none  [the longest x16 115 us: pair_sums(): jnp.sum(strength * (drift_three - radial * delta_three), axis=1)]
    pallas_call x0 -> x4, Pallas kernels: none -> 103 us  [the longest x1 57.7 us: body(): pl.pallas_call(pair_kernel, out_shape=shape((TEAMS, 2, 128), F32), in_spe...]
    ppermute x10 -> x0, starting transfers between devices: 41 us -> none  [shifted(): lax.ppermute(value, axis, [(i, (i + by) % size) for i in range(size)])]
    slice x33 -> x0, local copies, waits for them, and re-layouts: 26.3 us -> none  [the longest x32 25.7 us: pair_sums(): drift_one = sources[3][None, :] - targets[3][:, None]]
    psum x1 -> x0, blocking collectives: 19.8 us -> none  [replica_total(): return lax.psum(sums, 'rep')]
    ppermute x10 -> x0, waiting for transfers between devices: 7.61 us -> none  [shifted(): lax.ppermute(value, axis, [(i, (i + by) % size) for i in range(size)])]
    another operation x24 -> x0, local copies, waits for them, and re-layouts: 5.31 us -> none
    unnamed x4 -> x12, local copies, waits for them, and re-layouts: 0.01 us -> 4.93 us
  transfers between devices with their start and end apart: 10 -> 0, of which waited for: 3 -> 0; matrix products, arithmetic and copies ran while one was open for 58% -> 0% of each run, Pallas kernels for 0% -> 0%
where the time goes in v1:
time: 107 us; the launch traced here: 109 us
  Pallas kernels  103 us (96%)
  local copies, waits for them, and re-layouts  4.93 us (5%)
    pallas_call x1, Pallas kernels, body(): pl.pallas_call(pair_kernel, out_shape=shape((TEAMS, 2, 128), F32), in_spe...  57.7 us
    pallas_call x1, Pallas kernels, body(): pl.pallas_call(total_kernel, out_shape=(shape((3, CAP), F32), shape((3, C...  22.5 us
    pallas_call x1, Pallas kernels, body(): pl.pallas_call(share_kernel, out_shape=(shape((TEAMS, 2, 128), F32), shap...  20.5 us
    unnamed x12, local copies, waits for them, and re-layouts  4.93 us
    pallas_call x1, Pallas kernels, body(): pl.pallas_call(predict_kernel, out_shape=(shape((2, 128), F32), shape((8,...  2.19 us

profile of v1, /device:TPU:1, one launch (start us, length us, event | category | flops | bytes accessed | tf_op | source)
XLA Modules:
  0.0 108.5 jit_solution(16377413565789820237)
XLA Ops:
  0.6 2.2 %predict.1 = (f32[2,128]{1,0:T(2,128)}, f32[8,8192]{1,0:T(8,128)}) custom-call(s32[256]{0:T(256)} %index_ref.1, f32[3,8192]{1,0:T(4,128)} %pos.1, f32[3,8192]{1,0:T(4,128)} %vel.1, f32[3,8192]{1,0:T(4,128)} %acc.1, f32[3,8192]{1,0:T(4,128)} %jrk.1, f32[1,8192]{1,0:T(1,128)} %bitcast.3, f32[1,8192]{1,0:T(1,128)} %bitcast.4), custom_call_target="tpu_custom_call" | custom-call | tf_op jit(solution)/shard_map/predict/pallas_call | solution.py:334
  2.8 20.5 %share.1 = (f32[64,2,128]{2,1,0:T(2,128)}, s32[1,128]{1,0:T(1,128)}) custom-call(f32[2,128]{1,0:T(2,128)} %get-tuple-element.6.own), custom_call_target="tpu_custom_call" | custom-call | tf_op jit(solution)/shard_map/share/pallas_call | solution.py:341
  23.4 0.0 copy-start.3
  23.4 0.7 copy-done.3
  24.0 0.0 copy-start
  24.0 0.9 copy-done
  25.0 0.0 copy-start.2
  25.0 0.8 copy-done.2
  25.8 57.7 %pairs.1.partial = f32[64,2,128]{2,1,0:T(2,128)S(1)} custom-call(s32[1,128]{1,0:T(1,128)S(1)} %copy-done.3, f32[64,2,128]{2,1,0:T(2,128)S(1)} %copy-done.2, f32[8,8192]{1,0:T(8,128)S(1)} %copy-done), custom_call_target="tpu_custom_call" | custom-call | tf_op jit(solution)/shard_map/pairs/pallas_call | solution.py:350
  83.5 0.0 copy-start.1
  83.5 0.6 copy-done.1
  84.1 22.5 %totals.1 = (f32[3,256]{1,0:T(4,128)}, f32[3,256]{1,0:T(4,128)}) custom-call(f32[64,2,128]{2,1,0:T(2,128)} %copy-done.1, s32[1,256]{1,0:T(1,128)} %bitcast.5), custom_call_target="tpu_custom_call" | custom-call | tf_op jit(solution)/shard_map/totals/pallas_call | solution.py:368
  106.6 0.0 copy-start.4
  106.6 1.3 %copy.11 = f32[3,256]{1,0:T(4,128)} copy(f32[3,256]{1,0:T(4,128)} %get-tuple-element.12) | data formatting | bytes 6144
  107.9 0.0 copy-done.4
  107.9 0.6 copy.12
Async XLA Ops:
  23.4 0.7 copy-start.3
  24.0 0.9 copy-start
  25.0 0.8 copy-start.2
  83.5 0.6 copy-start.1
  106.6 1.3 %copy-start.4 = (f32[3,256]{1,0:T(4,128)S(1)}, f32[3,256]{1,0:T(4,128)}, u32[]{:S(2)}) copy-start(f32[3,256]{1,0:T(4,128)} %get-tuple-element.13) | copy-start | bytes 9220

commit v2 on v1

--- a/solution.py
+++ b/solution.py
@@ -18,7 +18,8 @@
 STARS_DEV = 8192
 MAX_ROWS = TEAMS * SHARE
 TB = 64
-CHUNK = 1024
+GROUP = 16
+UNROLL = 8
 
 
 def iota(shape, dim):
@@ -113,7 +114,7 @@
     offset_out[...] = jnp.sum(before, axis=0, keepdims=True).astype(jnp.int32)
 
 
-def pair_kernel(offset, targets, field, partial, comp, comp_out, tb, ft, fs, bmat, sum_s, sum_t):
+def pair_kernel(offset, targets, field, partial, comp, comp_out, tb, bmat, sum_s, sum_t):
     lane = iota((8, 128), 1)
     sub = iota((8, 128), 0)
     total = offset[0, TEAMS]
@@ -125,96 +126,111 @@
 
     lax.fori_loop(0, tiles + 2, clear, 0)
 
-    def compact(team, carry):
-        start = offset[0, team]
-        count = offset[0, team + 1] - start
-        message = targets[team]
-        rows = jnp.where(sub < 4, message[0:1, :], message[1:2, :])
-        rows = fanned(rows, 96)
-        rows = jnp.where(lane < count, rows, 0.0)
-        shift = lax.rem(start, 128)
-        rows = pltpu.roll(rows, shift, 1)
-        first = pl.multiple_of(lax.div(start, 128) * 128, 128)
-        comp[:, pl.ds(first, 128)] += jnp.where(lane >= shift, rows, 0.0)
-        comp[:, pl.ds(first + 128, 128)] += jnp.where(lane < shift, rows, 0.0)
-        return carry
-
-    lax.fori_loop(0, TEAMS, compact, 0)
+    def compact(step, carry):
+        ready = []
+        for k in range(UNROLL):
+            team = step * UNROLL + k
+            start = offset[0, team]
+            count = offset[0, team + 1] - start
+            message = targets[team]
+            rows = jnp.where(sub < 4, message[0:1, :], message[1:2, :])
+            rows = jnp.where(lane < count, fanned(rows, 96), 0.0)
+            shift = lax.rem(start, 128)
+            ready.append((pl.multiple_of(lax.div(start, 128) * 128, 128), shift, pltpu.roll(rows, shift, 1)))
+        for first, shift, rows in ready:
+            comp[:, pl.ds(first, 128)] += jnp.where(lane >= shift, rows, 0.0)
+            comp[:, pl.ds(first + 128, 128)] += jnp.where(lane < shift, rows, 0.0)
+        return carry
+
+    lax.fori_loop(0, TEAMS // UNROLL, compact, 0)
 
     def target_tile(tile, carry):
         at = pl.multiple_of(tile * 128, 128)
         rows = comp[:, pl.ds(at, 128)]
-        for k in range(3):
+        for k in range(6):
             tb[k, pl.ds(at, 128), :] = jnp.transpose(jnp.broadcast_to(rows[k : k + 1, :], (128, 128)))
-        inner = rows[0:1] * rows[3:4] + rows[1:2] * rows[4:5] + rows[2:3] * rows[5:6]
-        y = jnp.concatenate([-rows[3:6], -rows[0:3], jnp.ones((1, 128), F32), inner], 0)
-        a, b, c = (part.astype(F32) for part in split3(y))
-        stack = jnp.concatenate([a, b, a, b, c, a, jnp.zeros((80, 128), F32)], 0)
-        ft[pl.ds(at, 128), :] = jnp.transpose(stack).astype(BF16)
         return carry
 
     lax.fori_loop(0, tiles, target_tile, 0)
 
-    def source_tile(tile, carry):
-        at = pl.multiple_of(tile * 128, 128)
-        rows = field[:, pl.ds(at, 128)]
-        inner = rows[0:1] * rows[3:4] + rows[1:2] * rows[4:5] + rows[2:3] * rows[5:6]
-        x = jnp.concatenate([rows[0:6], inner, jnp.ones((1, 128), F32)], 0)
-        a, b, c = (part.astype(F32) for part in split3(x))
-        stack = jnp.concatenate([a, a, b, b, a, c, jnp.zeros((80, 128), F32)], 0)
-        fs[:, pl.ds(at, 128)] = stack.astype(BF16)
-        weighted = jnp.where(sub < 6, rows * rows[6:7, :], rows)
-        a, b, c = (part.astype(F32) for part in split3(weighted))
-        stack = jnp.concatenate([a, b, c, jnp.zeros((104, 128), F32)], 0)
-        bmat[pl.ds(at, 128), :] = jnp.transpose(stack).astype(BF16)
-        return carry
-
-    lax.fori_loop(0, STARS_DEV // 128, source_tile, 0)
-
-    def block(number, carry):
-        at = pl.multiple_of(number * TB, TB)
-
-        def chunk(step, sums):
-            base = pl.multiple_of(step * CHUNK, CHUNK)
-            twist = jnp.dot(ft[pl.ds(at, TB), :], fs[:, pl.ds(base, CHUNK)], preferred_element_type=F32)
-            left = []
-            for k in range(CHUNK // 256):
-                parts = [[], [], [], []]
-                for g in range(TB // 16):
-                    halves = []
-                    for m in range(2):
-                        cols = pl.ds(base + k * 256 + m * 128, 128)
-                        d = [field[c : c + 1, cols] - tb[c, pl.ds(at + g * 16, 16), :] for c in range(3)]
+    def source_tile(step, carry):
+        for k in range(4):
+            at = pl.multiple_of(step * 512 + k * 128, 128)
+            rows = field[:, pl.ds(at, 128)]
+            weighted = jnp.where(sub < 6, rows * rows[6:7, :], rows)
+            a, b, c = (part.astype(F32) for part in split3(weighted))
+            stack = jnp.concatenate([a, b, c, jnp.zeros((8, 128), F32)], 0)
+            bmat[pl.ds(at, 128), 0:32] = jnp.transpose(stack).astype(BF16)
+        return carry
+
+    lax.fori_loop(0, STARS_DEV // 512, source_tile, 0)
+
+    def with_accumulators(*accs):
+        groups = TB // GROUP
+        acc_s = [accs[m * groups : (m + 1) * groups] for m in range(2)]
+        acc_t = [accs[(2 + m) * groups : (3 + m) * groups] for m in range(2)]
+
+        def stage(chunk, register):
+            for m in range(2):
+                cols = pl.ds(pl.multiple_of(chunk * 512 + m * 256, 256), 256)
+                pltpu.matmul_push_rhs(bmat[cols, :], register, m)
+
+        def add_chunk(at, chunk, register):
+            for g in range(groups):
+                rows = pl.ds(at + g * GROUP, GROUP)
+                for m in range(2):
+                    parts = [[], [], [], []]
+                    for half in range(2):
+                        cols = pl.ds(pl.multiple_of(chunk * 512 + m * 256 + half * 128, 128), 128)
+                        d = [field[c : c + 1, cols] - tb[c, rows, :] for c in range(3)]
+                        w = [field[c + 3 : c + 4, cols] - tb[c + 3, rows, :] for c in range(3)]
                         r2 = d[0] * d[0] + d[1] * d[1] + d[2] * d[2] + SOFTENING
                         q = lax.rsqrt(r2)
+                        u = d[0] * w[0] + d[1] * w[1] + d[2] * w[2]
                         q2 = q * q
                         s = q * q2
-                        u = twist[g * 16 : g * 16 + 16, k * 256 + m * 128 : k * 256 + m * 128 + 128]
                         t = (u * q2) * s
                         s_hi, t_hi = s.astype(BF16), t.astype(BF16)
-                        s_lo = (s - s_hi.astype(F32)).astype(BF16)
-                        t_lo = (t - t_hi.astype(F32)).astype(BF16)
-                        halves.append((s_hi, t_hi, s_lo, t_lo))
-                    for n in range(4):
-                        parts[n].append(jnp.concatenate([halves[0][n], halves[1][n]], 1))
-                hi = jnp.concatenate(parts[0] + parts[1], 0)
-                lo = jnp.concatenate(parts[2] + parts[3], 0)
-                left += [hi, lo]
-            right = []
-            for k in range(CHUNK // 256):
-                b = bmat[pl.ds(base + k * 256, 256), :]
-                right += [b, b]
-            out = jnp.dot(
-                jnp.concatenate(left, 1), jnp.concatenate(right, 0), preferred_element_type=F32
-            )
-            return sums + out
-
-        sums = lax.fori_loop(0, STARS_DEV // CHUNK, chunk, jnp.zeros((2 * TB, 128), F32))
-        sum_s[pl.ds(at, TB), :] = sums[:TB]
-        sum_t[pl.ds(at, TB), :] = sums[TB:]
-        return carry
-
-    lax.fori_loop(0, lax.div(total + TB - 1, TB), block, 0)
+                        parts[0].append(s_hi)
+                        parts[1].append((s - s_hi.astype(F32)).astype(BF16))
+                        parts[2].append(t_hi)
+                        parts[3].append((t - t_hi.astype(F32)).astype(BF16))
+                    parts = [jnp.concatenate(pair, 1) for pair in parts]
+                    first = register if g == 0 else None
+                    pltpu.matmul_acc_lhs(acc_s[m][g], parts[0], load_staged_rhs=first)
+                    pltpu.matmul_acc_lhs(acc_s[m][g], parts[1])
+                    pltpu.matmul_acc_lhs(acc_t[m][g], parts[2])
+                    pltpu.matmul_acc_lhs(acc_t[m][g], parts[3])
+
+        chunks = STARS_DEV // 512
+
+        def block(number, carry):
+            at = pl.multiple_of(number * TB, TB)
+            stage(0, 0)
+
+            def two_chunks(step, inner):
+                for k in range(2):
+                    chunk = step * 2 + k
+                    stage(jnp.minimum(chunk + 1, chunks - 1), 1 - k)
+                    add_chunk(at, chunk, k)
+                return inner
+
+            lax.fori_loop(0, chunks // 2, two_chunks, 0)
+            for g in range(groups):
+                rows = pl.ds(at + g * GROUP, GROUP)
+                sum_s[rows, :] = pltpu.matmul_pop(acc_s[0][g])[:, :128] + pltpu.matmul_pop(acc_s[1][g])[:, :128]
+                sum_t[rows, :] = pltpu.matmul_pop(acc_t[0][g])[:, :128] + pltpu.matmul_pop(acc_t[1][g])[:, :128]
+            for m in range(2):
+                pltpu.matmul_acc_lhs(acc_s[m][0], jnp.zeros((GROUP, 256), BF16), load_staged_rhs=0)
+                pltpu.matmul_pop(acc_s[m][0])
+            return carry
+
+        lax.fori_loop(0, lax.div(total + TB - 1, TB), block, 0)
+
+    sets = []
+    for m in (0, 1, 0, 1):
+        sets += [pltpu.ACC(m)((GROUP, 256), F32)] * (TB // GROUP)
+    pl.run_scoped(with_accumulators, *sets)
 
     def result_tile(tile, carry):
         at = pl.multiple_of(tile * 128, 128)
@@ -233,22 +249,23 @@
 
     lax.fori_loop(0, tiles, result_tile, 0)
 
-    def expand(team, carry):
-        start = offset[0, team]
-        count = offset[0, team + 1] - start
-        shift = lax.rem(start, 128)
-        first = pl.multiple_of(lax.div(start, 128) * 128, 128)
-        both = jnp.where(lane >= shift, comp_out[:, pl.ds(first, 128)], comp_out[:, pl.ds(first + 128, 128)])
-        rows = pltpu.roll(both, lax.rem(128 - shift, 128), 1)
-        rows = jnp.where(lane < count, rows, 0.0)
-        rows = fanned(rows, 32)
-        rows = jnp.where(lane // 32 == lax.rem(sub, 4), rows, 0.0)
-        partial[team] = jnp.concatenate(
-            [jnp.sum(rows[0:4], axis=0, keepdims=True), jnp.sum(rows[4:8], axis=0, keepdims=True)], 0
-        )
-        return carry
-
-    lax.fori_loop(0, TEAMS, expand, 0)
+    def expand(step, carry):
+        for k in range(UNROLL):
+            team = step * UNROLL + k
+            start = offset[0, team]
+            count = offset[0, team + 1] - start
+            shift = lax.rem(start, 128)
+            first = pl.multiple_of(lax.div(start, 128) * 128, 128)
+            both = jnp.where(lane >= shift, comp_out[:, pl.ds(first, 128)], comp_out[:, pl.ds(first + 128, 128)])
+            rows = pltpu.roll(both, lax.rem(128 - shift, 128), 1)
+            rows = fanned(jnp.where(lane < count, rows, 0.0), 32)
+            rows = rows + pltpu.roll(rows, 6, 0)
+            rows = rows + pltpu.roll(rows, 7, 0)
+            partial[team, 0:1, :] = rows[0:1, :]
+            partial[team, 1:2, :] = rows[4:5, :]
+        return carry
+
+    lax.fori_loop(0, TEAMS // UNROLL, expand, 0)
 
 
 def total_kernel(partial, live, force, new_jerk, recv, mine, ring, send_sem, recv_sem, send_sem2, recv_sem2):
@@ -327,6 +344,26 @@
     return pl.BlockSpec(memory_space=pltpu.SMEM)
 
 
+def pairs(offset, targets, field):
+    shape = jax.ShapeDtypeStruct
+    return pl.pallas_call(
+        pair_kernel,
+        out_shape=shape((TEAMS, 2, 128), F32),
+        in_specs=[in_smem(), in_vmem(), in_vmem()],
+        out_specs=in_vmem(),
+        scratch_shapes=[
+            pltpu.VMEM((8, MAX_ROWS + 256), F32),
+            pltpu.VMEM((8, MAX_ROWS + 256), F32),
+            pltpu.VMEM((6, MAX_ROWS, 128), F32),
+            pltpu.VMEM((STARS_DEV, 256), BF16),
+            pltpu.VMEM((MAX_ROWS, 128), F32),
+            pltpu.VMEM((MAX_ROWS, 128), F32),
+        ],
+        compiler_params=pltpu.CompilerParams(vmem_limit_bytes=32 * 2**20),
+        name="pairs",
+    )(offset, targets, field)
+
+
 def body(position, velocity, accel, jerk, mass, elapsed, active_index):
     shape = jax.ShapeDtypeStruct
     message = pltpu.VMEM((TEAMS, 2, 128), F32)
@@ -347,24 +384,7 @@
         compiler_params=pltpu.CompilerParams(collective_id=0, has_side_effects=True),
         name="share",
     )(own)
-    partial = pl.pallas_call(
-        pair_kernel,
-        out_shape=shape((TEAMS, 2, 128), F32),
-        in_specs=[in_smem(), in_vmem(), in_vmem()],
-        out_specs=in_vmem(),
-        scratch_shapes=[
-            pltpu.VMEM((8, MAX_ROWS + 256), F32),
-            pltpu.VMEM((8, MAX_ROWS + 256), F32),
-            pltpu.VMEM((3, MAX_ROWS, 128), F32),
-            pltpu.VMEM((MAX_ROWS, 128), BF16),
-            pltpu.VMEM((128, STARS_DEV), BF16),
-            pltpu.VMEM((STARS_DEV, 128), BF16),
-            pltpu.VMEM((MAX_ROWS, 128), F32),
-            pltpu.VMEM((MAX_ROWS, 128), F32),
-        ],
-        compiler_params=pltpu.CompilerParams(vmem_limit_bytes=48 * 2**20),
-        name="pairs",
-    )(offset, targets, field)
+    partial = pairs(offset, targets, field)
     return pl.pallas_call(
         total_kernel,
         out_shape=(shape((3, CAP), F32), shape((3, CAP), F32)),

time: 107 us -> 81.9 us (0.77); the launches traced: 109 us -> 81.6 us
  Pallas kernels: 103 us -> 76 us
    pallas_call x1, Pallas kernels: 57.7 us -> 30.8 us  [pairs(): pl.pallas_call(pair_kernel, out_shape=shape((TEAMS, 2, 128), F32), in_spe...]
where the time goes in v2:
time: 81.9 us; the launch traced here: 81.6 us
  Pallas kernels  76 us (93%)
  local copies, waits for them, and re-layouts  4.92 us (6%)
    pallas_call x1, Pallas kernels, pairs(): pl.pallas_call(pair_kernel, out_shape=shape((TEAMS, 2, 128), F32), in_spe...  30.8 us
    pallas_call x1, Pallas kernels, body(): pl.pallas_call(total_kernel, out_shape=(shape((3, CAP), F32), shape((3, C...  22.5 us
    pallas_call x1, Pallas kernels, body(): pl.pallas_call(share_kernel, out_shape=(shape((TEAMS, 2, 128), F32), shap...  20.5 us
    unnamed x12, local copies, waits for them, and re-layouts  4.92 us
    pallas_call x1, Pallas kernels, body(): pl.pallas_call(predict_kernel, out_shape=(shape((2, 128), F32), shape((8,...  2.19 us

profile of v2, /device:TPU:1, one launch (start us, length us, event | category | flops | bytes accessed | tf_op | source)
XLA Modules:
  0.0 81.6 jit_solution(593728534479324648)
XLA Ops:
  0.6 2.2 %predict.1 = (f32[2,128]{1,0:T(2,128)}, f32[8,8192]{1,0:T(8,128)}) custom-call(s32[256]{0:T(256)} %index_ref.1, f32[3,8192]{1,0:T(4,128)} %pos.1, f32[3,8192]{1,0:T(4,128)} %vel.1, f32[3,8192]{1,0:T(4,128)} %acc.1, f32[3,8192]{1,0:T(4,128)} %jrk.1, f32[1,8192]{1,0:T(1,128)} %bitcast.3, f32[1,8192]{1,0:T(1,128)} %bitcast.4), custom_call_target="tpu_custom_call" | custom-call | tf_op jit(solution)/shard_map/predict/pallas_call | solution.py:371
  2.8 20.5 %share.1 = (f32[64,2,128]{2,1,0:T(2,128)}, s32[1,128]{1,0:T(1,128)}) custom-call(f32[2,128]{1,0:T(2,128)} %get-tuple-element.6.own), custom_call_target="tpu_custom_call" | custom-call | tf_op jit(solution)/shard_map/share/pallas_call | solution.py:378
  23.4 0.0 copy-start.3
  23.4 0.7 copy-done.3
  24.0 0.0 copy-start
  24.0 0.9 %copy-done = f32[8,8192]{1,0:T(8,128)S(1)} copy-done((f32[8,8192]{1,0:T(8,128)S(1)}, f32[8,8192]{1,0:T(8,128)}, u32[]{:S(2)}) %copy-start) | copy-done | bytes 262168
  25.0 0.0 copy-start.2
  25.0 0.8 %copy-done.2 = f32[64,2,128]{2,1,0:T(2,128)S(1)} copy-done((f32[64,2,128]{2,1,0:T(2,128)S(1)}, f32[64,2,128]{2,1,0:T(2,128)}, u32[]{:S(2)}) %copy-start.2) | copy-done | bytes 65560
  25.8 30.8 %pairs.1.partial = f32[64,2,128]{2,1,0:T(2,128)S(1)} custom-call(s32[1,128]{1,0:T(1,128)S(1)} %copy-done.3, f32[64,2,128]{2,1,0:T(2,128)S(1)} %copy-done.2, f32[8,8192]{1,0:T(8,128)S(1)} %copy-done), custom_call_target="tpu_custom_call" | custom-call | tf_op jit(solution)/shard_map/pairs/pallas_call | solution.py:349
  56.6 0.0 copy-start.1
  56.6 0.6 copy-done.1
  57.2 22.5 %totals.1 = (f32[3,256]{1,0:T(4,128)}, f32[3,256]{1,0:T(4,128)}) custom-call(f32[64,2,128]{2,1,0:T(2,128)} %copy-done.1, s32[1,256]{1,0:T(1,128)} %bitcast.5), custom_call_target="tpu_custom_call" | custom-call | tf_op jit(solution)/shard_map/totals/pallas_call | solution.py:388
  79.7 0.0 copy-start.4
  79.7 1.3 %copy.11 = f32[3,256]{1,0:T(4,128)} copy(f32[3,256]{1,0:T(4,128)} %get-tuple-element.12) | data formatting | bytes 6144
  81.0 0.0 copy-done.4
  81.0 0.6 copy.12
Async XLA Ops:
  23.4 0.7 copy-start.3
  24.0 0.9 %copy-start = (f32[8,8192]{1,0:T(8,128)S(1)}, f32[8,8192]{1,0:T(8,128)}, u32[]{:S(2)}) copy-start(f32[8,8192]{1,0:T(8,128)} %get-tuple-element.9.field) | copy-start | bytes 786436
  25.0 0.8 %copy-start.2 = (f32[64,2,128]{2,1,0:T(2,128)S(1)}, f32[64,2,128]{2,1,0:T(2,128)}, u32[]{:S(2)}) copy-start(f32[64,2,128]{2,1,0:T(2,128)} %get-tuple-element.8.targets) | copy-start | bytes 196612
  56.6 0.6 copy-start.1
  79.7 1.3 %copy-start.4 = (f32[3,256]{1,0:T(4,128)S(1)}, f32[3,256]{1,0:T(4,128)}, u32[]{:S(2)}) copy-start(f32[3,256]{1,0:T(4,128)} %get-tuple-element.13) | copy-start | bytes 9220

commit v3 on v2

--- a/solution.py
+++ b/solution.py
@@ -56,39 +56,87 @@
     lax.fori_loop(1, size, one, 0)
 
 
-def predict_kernel(index_ref, pos, vel, acc, jrk, mass, elapsed, own, field):
+def copy_all(pairs, sems):
+    copies = [pltpu.make_async_copy(src, dst, sems.at[k]) for k, (src, dst) in enumerate(pairs)]
+    for copy in copies:
+        copy.start()
+    return copies
+
+
+def share_kernel(
+    index_ref,
+    pos_hbm,
+    vel_hbm,
+    acc_hbm,
+    jrk_hbm,
+    mass_hbm,
+    elapsed_hbm,
+    targets_out,
+    offset_out,
+    field_hbm,
+    columns_hbm,
+    pos,
+    vel,
+    acc,
+    jrk,
+    mass,
+    elapsed,
+    field,
+    columns,
+    own,
+    recv,
+    load_sem,
+    store_sem,
+    send_sem,
+    recv_sem,
+):
     team = lax.axis_index("blk")
     rep = lax.axis_index("rep")
+    barrier = pltpu.get_barrier_semaphore()
+    loads = copy_all(
+        [(pos_hbm, pos), (vel_hbm, vel), (acc_hbm, acc), (jrk_hbm, jrk), (mass_hbm, mass), (elapsed_hbm, elapsed)],
+        load_sem,
+    )
+    signal_peers(barrier, "blk", team, TEAMS)
+    for copy in loads:
+        copy.wait()
+
     h = elapsed[...]
     v, a, j = vel[...], acc[...], jrk[...]
     field[0:3, :] = pos[...] + h * (v + h * (0.5 * a + h / 6.0 * j))
     field[3:6, :] = v + h * (a + 0.5 * h * j)
-    field[6:7, :] = jnp.ones((1, STARS_DEV), F32)
-    field[7:8, :] = jnp.zeros((1, STARS_DEV), F32)
+    field[6:7, :] = mass[...]
+    field[7:8, :] = jnp.ones((1, STARS_DEV), F32)
+    stores = [pltpu.make_async_copy(field, field_hbm, store_sem.at[0])]
+    stores[0].start()
 
     phase = phase_of(team, rep)
     lane = iota((8, 128), 1)
     sub = iota((8, 128), 0)
     picked = jnp.zeros((8, 128), F32)
-    for k in range(SHARE):
-        index = index_ref[REPS * k + phase]
-        local = jnp.clip(index - team * STARS_DEV, 0, STARS_DEV - 1)
-        tile = field[:, pl.ds(pl.multiple_of(lax.div(local, 128) * 128, 128), 128)]
-        turned = pltpu.roll(tile, lax.rem(k - lax.rem(local, 128) + 128, 128), 1)
-        picked = jnp.where((lane == k) & (index >= 0), turned, picked)
-    spread = fanned(picked, 32)
-    spread = jnp.where(lane // 32 == lax.rem(sub, 4), spread, 0.0)
-    own[...] = jnp.concatenate(
-        [jnp.sum(spread[0:4], axis=0, keepdims=True), jnp.sum(spread[4:8], axis=0, keepdims=True)], 0
-    )
-    field[6:7, :] = mass[...]
-
-
-def share_kernel(own, targets_out, offset_out, recv, send_sem, recv_sem):
-    team = lax.axis_index("blk")
-    barrier = pltpu.get_barrier_semaphore()
-    signal_peers(barrier, "blk", team, TEAMS)
-    recv[team] = own[...]
+    for group in range(2):
+        slots = range(group * 16, group * 16 + 16)
+        local = [index_ref[REPS * k + phase] - team * STARS_DEV for k in slots]
+
+        def look(step, found):
+            for k in range(4):
+                at = pl.multiple_of(step * 512 + k * 128, 128)
+                tile = field[:, pl.ds(at, 128)]
+                number = lane + at
+                found = tuple(jnp.where(number == want, tile, old) for want, old in zip(local, found))
+            return found
+
+        found = lax.fori_loop(0, STARS_DEV // 512, look, (jnp.zeros((8, 128), F32),) * 16)
+        for k, one in zip(slots, found):
+            picked = jnp.where(lane == k, jnp.sum(one, axis=1, keepdims=True), picked)
+    picked = jnp.where(sub == 6, pltpu.roll(picked, 7, 0), picked)
+    spread = fanned(jnp.where(lane < SHARE, picked, 0.0), 32)
+    spread = spread + pltpu.roll(spread, 6, 0)
+    spread = spread + pltpu.roll(spread, 7, 0)
+    own[0:1, :] = spread[0:1, :]
+    own[1:2, :] = spread[4:5, :]
+    recv[team] = jnp.concatenate([spread[0:1, :], spread[4:5, :]], 0)
+
     pl.semaphore_wait(barrier, TEAMS - 1)
 
     def send(step, carry):
@@ -103,6 +151,20 @@
         return carry
 
     lax.fori_loop(1, TEAMS, send, 0)
+
+    def source_tile(step, carry):
+        for k in range(4):
+            at = pl.multiple_of(step * 512 + k * 128, 128)
+            rows = field[:, pl.ds(at, 128)]
+            weighted = jnp.where(sub < 6, rows * rows[6:7, :], rows)
+            a, b, c = (part.astype(F32) for part in split3(weighted))
+            stack = jnp.concatenate([a, b, c, jnp.zeros((104, 128), F32)], 0)
+            columns[pl.ds(at, 128), :] = jnp.transpose(stack).astype(BF16)
+        return carry
+
+    lax.fori_loop(0, STARS_DEV // 512, source_tile, 0)
+    stores.append(pltpu.make_async_copy(columns, columns_hbm, store_sem.at[1]))
+    stores[1].start()
     pltpu.make_async_copy(recv.at[pl.ds(0, TEAMS - 1)], recv.at[pl.ds(0, TEAMS - 1)], recv_sem).wait()
     pltpu.make_async_copy(recv.at[pl.ds(0, TEAMS - 1)], recv.at[pl.ds(0, TEAMS - 1)], send_sem).wait()
     got = recv[...]
@@ -112,11 +174,21 @@
     counts = jnp.sum(flags, axis=1, keepdims=True)
     before = jnp.where(iota((TEAMS, 128), 0) < flag_lanes, counts, 0.0)
     offset_out[...] = jnp.sum(before, axis=0, keepdims=True).astype(jnp.int32)
-
-
-def pair_kernel(offset, targets, field, partial, comp, comp_out, tb, bmat, sum_s, sum_t):
+    for copy in stores:
+        copy.wait()
+
+
+def pair_kernel(
+    offset_hbm, targets_hbm, field_hbm, columns_hbm, partial,
+    offset, targets, field, columns, load_sem, comp, comp_out, tb, sum_s, sum_t,
+):
+    loads = copy_all(
+        [(offset_hbm, offset), (targets_hbm, targets), (field_hbm, field), (columns_hbm, columns)], load_sem
+    )
     lane = iota((8, 128), 1)
     sub = iota((8, 128), 0)
+    loads[0].wait()
+    loads[1].wait()
     total = offset[0, TEAMS]
     tiles = lax.div(total + 127, 128)
 
@@ -153,17 +225,8 @@
 
     lax.fori_loop(0, tiles, target_tile, 0)
 
-    def source_tile(step, carry):
-        for k in range(4):
-            at = pl.multiple_of(step * 512 + k * 128, 128)
-            rows = field[:, pl.ds(at, 128)]
-            weighted = jnp.where(sub < 6, rows * rows[6:7, :], rows)
-            a, b, c = (part.astype(F32) for part in split3(weighted))
-            stack = jnp.concatenate([a, b, c, jnp.zeros((8, 128), F32)], 0)
-            bmat[pl.ds(at, 128), 0:32] = jnp.transpose(stack).astype(BF16)
-        return carry
-
-    lax.fori_loop(0, STARS_DEV // 512, source_tile, 0)
+    loads[2].wait()
+    loads[3].wait()
 
     def with_accumulators(*accs):
         groups = TB // GROUP
@@ -173,7 +236,8 @@
         def stage(chunk, register):
             for m in range(2):
                 cols = pl.ds(pl.multiple_of(chunk * 512 + m * 256, 256), 256)
-                pltpu.matmul_push_rhs(bmat[cols, :], register, m)
+                rhs = jnp.concatenate([columns[cols, :], jnp.zeros((256, 128), BF16)], 1)
+                pltpu.matmul_push_rhs(rhs, register, m)
 
         def add_chunk(at, chunk, register):
             for g in range(groups):
@@ -268,17 +332,19 @@
     lax.fori_loop(0, TEAMS // UNROLL, expand, 0)
 
 
-def total_kernel(partial, live, force, new_jerk, recv, mine, ring, send_sem, recv_sem, send_sem2, recv_sem2):
+def total_kernel(
+    partial_hbm, ring_out, partial, recv, mine, ring, load_sem, send_sem, recv_sem, send_sem2, recv_sem2
+):
     team = lax.axis_index("blk")
     rep = lax.axis_index("rep")
     barrier = pltpu.get_barrier_semaphore()
+    load = pltpu.make_async_copy(partial_hbm, partial, load_sem)
+    load.start()
     signal_peers(barrier, "blk", team, TEAMS)
     signal_peers(barrier, "rep", rep, REPS)
     phase = phase_of(team, rep)
+    load.wait()
     recv[team] = partial[team]
-    source = iota((CAP, CAP), 0)
-    slot = iota((CAP, CAP), 1)
-    place = jnp.where(slot == lax.rem(source, SHARE) * REPS + source // SHARE, 1.0, 0.0).astype(BF16)
     pl.semaphore_wait(barrier, TEAMS + REPS - 2)
 
     def send(step, carry):
@@ -314,6 +380,13 @@
     pltpu.make_async_copy(recv.at[pl.ds(0, TEAMS - 1)], recv.at[pl.ds(0, TEAMS - 1)], send_sem).wait()
     pltpu.make_async_copy(ring.at[pl.ds(0, REPS - 1)], ring.at[pl.ds(0, REPS - 1)], recv_sem2).wait()
     pltpu.make_async_copy(ring.at[pl.ds(0, REPS - 1)], ring.at[pl.ds(0, REPS - 1)], send_sem2).wait()
+    ring_out[...] = ring[...]
+
+
+def finish_kernel(ring, live, force, new_jerk):
+    source = iota((CAP, CAP), 0)
+    slot = iota((CAP, CAP), 1)
+    place = jnp.where(slot == lax.rem(source, SHARE) * REPS + lax.div(source, SHARE), 1.0, 0.0).astype(BF16)
     lane = iota((8, 128), 1)
     sub = iota((8, 128), 0)
     halves = []
@@ -344,56 +417,91 @@
     return pl.BlockSpec(memory_space=pltpu.SMEM)
 
 
-def pairs(offset, targets, field):
-    shape = jax.ShapeDtypeStruct
+def anywhere():
+    return pl.BlockSpec(memory_space=pl.ANY)
+
+
+def pairs(offset, targets, field, columns):
     return pl.pallas_call(
         pair_kernel,
-        out_shape=shape((TEAMS, 2, 128), F32),
-        in_specs=[in_smem(), in_vmem(), in_vmem()],
+        out_shape=jax.ShapeDtypeStruct((TEAMS, 2, 128), F32),
+        in_specs=[anywhere()] * 4,
         out_specs=in_vmem(),
         scratch_shapes=[
+            pltpu.SMEM((1, 128), jnp.int32),
+            pltpu.VMEM((TEAMS, 2, 128), F32),
+            pltpu.VMEM((8, STARS_DEV), F32),
+            pltpu.VMEM((STARS_DEV, 128), BF16),
+            pltpu.SemaphoreType.DMA((4,)),
             pltpu.VMEM((8, MAX_ROWS + 256), F32),
             pltpu.VMEM((8, MAX_ROWS + 256), F32),
             pltpu.VMEM((6, MAX_ROWS, 128), F32),
-            pltpu.VMEM((STARS_DEV, 256), BF16),
             pltpu.VMEM((MAX_ROWS, 128), F32),
             pltpu.VMEM((MAX_ROWS, 128), F32),
         ],
-        compiler_params=pltpu.CompilerParams(vmem_limit_bytes=32 * 2**20),
+        compiler_params=pltpu.CompilerParams(vmem_limit_bytes=56 * 2**20),
         name="pairs",
-    )(offset, targets, field)
+    )(offset, targets, field, columns)
 
 
 def body(position, velocity, accel, jerk, mass, elapsed, active_index):
     shape = jax.ShapeDtypeStruct
     message = pltpu.VMEM((TEAMS, 2, 128), F32)
+    row = pltpu.VMEM((1, STARS_DEV), F32)
+    triple = pltpu.VMEM((3, STARS_DEV), F32)
     dma = pltpu.SemaphoreType.DMA
-    own, field = pl.pallas_call(
-        predict_kernel,
-        out_shape=(shape((2, 128), F32), shape((8, STARS_DEV), F32)),
-        in_specs=[in_smem()] + [in_vmem()] * 6,
-        out_specs=(in_vmem(),) * 2,
-        name="predict",
+    targets, offset, field, columns = pl.pallas_call(
+        share_kernel,
+        out_shape=(
+            shape((TEAMS, 2, 128), F32),
+            shape((1, 128), jnp.int32),
+            shape((8, STARS_DEV), F32),
+            shape((STARS_DEV, 128), BF16),
+        ),
+        in_specs=[in_smem()] + [anywhere()] * 6,
+        out_specs=(in_vmem(), in_vmem(), anywhere(), anywhere()),
+        scratch_shapes=[triple] * 4
+        + [row] * 2
+        + [
+            pltpu.VMEM((8, STARS_DEV), F32),
+            pltpu.VMEM((STARS_DEV, 128), BF16),
+            pltpu.VMEM((2, 128), F32),
+            message,
+            dma((6,)),
+            dma((2,)),
+            dma,
+            dma,
+        ],
+        compiler_params=pltpu.CompilerParams(collective_id=0, has_side_effects=True, vmem_limit_bytes=56 * 2**20),
+        name="share",
     )(active_index, position, velocity, accel, jerk, mass[None, :], elapsed[None, :])
-    targets, offset = pl.pallas_call(
-        share_kernel,
-        out_shape=(shape((TEAMS, 2, 128), F32), shape((1, 128), jnp.int32)),
-        in_specs=[in_vmem()],
-        out_specs=(in_vmem(),) * 2,
-        scratch_shapes=[message, dma, dma],
-        compiler_params=pltpu.CompilerParams(collective_id=0, has_side_effects=True),
-        name="share",
-    )(own)
-    partial = pairs(offset, targets, field)
+    partial = pairs(offset, targets, field, columns)
+    ring = pl.pallas_call(
+        total_kernel,
+        out_shape=shape((REPS, 2, 128), F32),
+        in_specs=[anywhere()],
+        out_specs=in_vmem(),
+        scratch_shapes=[
+            message,
+            message,
+            pltpu.VMEM((2, 128), F32),
+            pltpu.VMEM((REPS, 2, 128), F32),
+            dma,
+            dma,
+            dma,
+            dma,
+            dma,
+        ],
+        compiler_params=pltpu.CompilerParams(collective_id=1, has_side_effects=True),
+        name="totals",
+    )(partial)
     return pl.pallas_call(
-        total_kernel,
+        finish_kernel,
         out_shape=(shape((3, CAP), F32), shape((3, CAP), F32)),
         in_specs=[in_vmem(), in_vmem()],
         out_specs=(in_vmem(),) * 2,
-        scratch_shapes=[message, pltpu.VMEM((2, 128), F32), pltpu.VMEM((REPS, 2, 128), F32), dma, dma, dma, dma],
-        compiler_params=pltpu.CompilerParams(collective_id=1, has_side_effects=True),
-        name="totals",
-    )(partial, active_index[None, :])
+        name="finish",
+    )(ring, active_index[None, :])
 
 
 def solution(mesh):

time: 81.9 us -> 70.8 us (0.86)
  Pallas kernels: 76 us -> 69.9 us
  local copies, waits for them, and re-layouts: 4.92 us -> 0 us
    pallas_call x3, Pallas kernels: 55.5 us -> 48.9 us  [the longest x1 25.7 us: pairs(): pl.pallas_call(pair_kernel, out_shape=jax.ShapeDtypeStruct((TEAMS, 2, 128...]
    unnamed x12 -> x0, local copies, waits for them, and re-layouts: 4.92 us -> none
where the time goes in v3:
time: 70.8 us; the launch traced here: 70.6 us
  Pallas kernels  69.9 us (99%)
    pallas_call x1, Pallas kernels, pairs(): pl.pallas_call(pair_kernel, out_shape=jax.ShapeDtypeStruct((TEAMS, 2, 128...  25.7 us
    pallas_call x1, Pallas kernels, body(): pl.pallas_call(total_kernel, out_shape=shape((REPS, 2, 128), F32), in_spe...  21.7 us
    pallas_call x1, Pallas kernels, body(): pl.pallas_call(share_kernel, out_shape=(shape((TEAMS, 2, 128), F32), shap...  21 us
    pallas_call x1, Pallas kernels, body(): pl.pallas_call(finish_kernel, out_shape=(shape((3, CAP), F32), shape((3,...  1.58 us

profile of v3, /device:TPU:1, one launch (start us, length us, event | category | flops | bytes accessed | tf_op | source)
XLA Modules:
  0.0 70.6 jit_solution(14455645101817937124)
XLA Ops:
  0.6 21.0 %share.1 = (f32[64,2,128]{2,1,0:T(2,128)}, s32[1,128]{1,0:T(1,128)}, f32[8,8192]{1,0:T(8,128)}, bf16[8192,128]{1,0:T(8,128)(2,1)}) custom-call(s32[256]{0:T(256)} %index_ref.1, f32[3,8192]{1,0:T(4,128)} %pos_hbm.1, f32[3,8192]{1,0:T(4,128)} %vel_hbm.1, f32[3,8192]{1,0:T(4,128)} %acc_hbm.1, f32[3,8192]{1,0:T(4,128)} %jrk_hbm.1, f32[1,8192]{1,0:T(1,128)} %bitcast.3, ...), custom_call_target="tpu_custom_call" | custom-call | tf_op jit(solution)/shard_map/share/pallas_call | solution.py:453
  21.6 25.7 %pairs.1.partial_hbm = f32[64,2,128]{2,1,0:T(2,128)} custom-call(s32[1,128]{1,0:T(1,128)} %get-tuple-element.6.offset_hbm, f32[64,2,128]{2,1,0:T(2,128)} %get-tuple-element.7.targets_hbm, f32[8,8192]{1,0:T(8,128)} %get-tuple-element.8.field_hbm, bf16[8192,128]{1,0:T(8,128)(2,1)} %get-tuple-element.9.columns_hbm), custom_call_target="tpu_custom_call" | custom-call | tf_op jit(solution)/shard_map/pairs/pallas_call | solution.py:425
  47.2 21.7 %totals.1.ring = f32[8,2,128]{2,1,0:T(2,128)} custom-call(f32[64,2,128]{2,1,0:T(2,128)} %pairs.1.partial_hbm), custom_call_target="tpu_custom_call" | custom-call | tf_op jit(solution)/shard_map/totals/pallas_call | solution.py:479
  69.0 1.6 %finish.1 = (f32[3,256]{1,0:T(4,128)}, f32[3,256]{1,0:T(4,128)}) custom-call(f32[8,2,128]{2,1,0:T(2,128)} %totals.1.ring, s32[1,256]{1,0:T(1,128)} %bitcast.5), custom_call_target="tpu_custom_call" | custom-call | tf_op jit(solution)/shard_map/finish/pallas_call | solution.py:498
